TPU v7x, 512 devices: a whole 4x4x16 slice. The times are simulated.
512 devices in a mesh: samp: 32 (over y_hi, z), head: 16 (over y_lo, x, core).
Axes of the slice: x: 4, y: 4 (y_hi: 2, y_lo: 2; y = y_hi * 2 + y_lo), z: 16, core: 2. Of those that a mesh axis runs over, the one named last changes fastest.
Arguments:
- queries: bfloat16 [32, 768, 512], P('samp', 'head'), may hold values from -10 to 10
- keys: bfloat16 [32, 768, 512], P('samp', 'head'), may hold values from -10 to 10
- values: bfloat16 [32, 768, 512], P('samp', 'head'), may hold values from -6 to 6
- out_grad: bfloat16 [32, 768, 512], P('samp', 'head'), may hold values from -6 to 6
- pair: bfloat16 [512, 512, 128], P('head', 'samp'), may hold values from -6 to 6
- ln_gain: float32 [128], replicated, may hold values from 0.25 to 1.75
- proj_weight: bfloat16 [128, 16], replicated, may hold values from -0.5 to 0.5
- token_mask: int32 [512], replicated, may hold values from 0 to 1, as said below
- atom_map: int32 [4096], replicated, may hold values from 0 to 511, never falling along the last dimension, each value on 1 to 24 neighbouring positions
Outputs:
- attended: bfloat16 [32, 768, 512], P('samp', 'head')
- query_grad: bfloat16 [32, 768, 512], P('samp', 'head')
- key_grad: bfloat16 [32, 768, 512], P('samp', 'head')
- value_grad: bfloat16 [32, 768, 512], P('samp', 'head')
- pair_grad: bfloat16 [512, 512, 128], P('head', 'samp')
- weight_grad: float32 [128, 16], replicated
- gain_grad: float32 [128], replicated
Inputs may be any that keep to these rules, and one draw needn't show every extreme that they name: `token_mask`: real tokens form a prefix of 256 or more tokens; the last token is padding.
All inputs are finite; a program needn't handle non-finite values.
Results may differ from a plain program's by a relative error of at most 0.02.
Values may be sent and summed in bfloat16 or wider, within the bound.
A program may use at most 64 MiB of HBM per device.

v0:
```python
import jax
import jax.numpy as jnp
from jax import lax
from jax.sharding import PartitionSpec as P


def token_weights(atom_map, token_mask):
    count = token_mask.shape[0]
    ends = jnp.searchsorted(atom_map, jnp.arange(count, dtype=jnp.int32), side="right")
    starts = jnp.concatenate([jnp.zeros((1,), jnp.int32), ends[:-1]])
    return (
        (ends - starts).astype(jnp.float32)
        * (count / atom_map.shape[0])
        * token_mask.astype(jnp.float32)
    )


def attend(query_row, key_row, value_row, grad_row, bias, key_keep, tok_weight):
    count = query_row.shape[1]
    local_heads = bias.shape[0]
    query_h = query_row.reshape(local_heads, -1, count)
    key_h = key_row.reshape(local_heads, -1, count)
    value_h = value_row.reshape(local_heads, -1, count)
    inv_root = 1.0 / jnp.sqrt(jnp.float32(query_h.shape[1]))
    scores = jnp.einsum(
        "hdi,hdj->hij", query_h, key_h, preferred_element_type=jnp.float32
    ) * inv_root + bias.astype(jnp.float32)
    scores = jnp.where(key_keep[None, None, :], scores, jnp.float32(-1000000000.0))
    largest = jnp.max(scores, axis=-1, keepdims=True)
    expo = jnp.exp(scores - largest)
    prob = expo / jnp.sum(expo, axis=-1, keepdims=True)
    prob_b = prob.astype(jnp.bfloat16)
    attended = jnp.einsum(
        "hij,hdj->hdi", prob_b, value_h, preferred_element_type=jnp.float32
    ).astype(jnp.bfloat16)
    grad_in = (grad_row.astype(jnp.float32) * tok_weight[None, :]).astype(jnp.bfloat16)
    grad_h = grad_in.reshape(local_heads, -1, count)
    dprob = jnp.einsum("hdi,hdj->hij", grad_h, value_h, preferred_element_type=jnp.float32)
    row_dot = jnp.sum(prob * dprob, axis=-1, keepdims=True)
    dscore = prob * (dprob - row_dot)
    dscore_b = dscore.astype(jnp.bfloat16)
    query_grad = (
        jnp.einsum("hij,hdj->hdi", dscore_b, key_h, preferred_element_type=jnp.float32) * inv_root
    ).astype(jnp.bfloat16)
    key_grad = (
        jnp.einsum("hij,hdi->hdj", dscore_b, query_h, preferred_element_type=jnp.float32) * inv_root
    ).astype(jnp.bfloat16)
    value_grad = jnp.einsum(
        "hij,hdi->hdj", prob_b, grad_h, preferred_element_type=jnp.float32
    ).astype(jnp.bfloat16)
    shape = (-1, count)
    return (
        attended.reshape(shape),
        query_grad.reshape(shape),
        key_grad.reshape(shape),
        value_grad.reshape(shape),
        dscore,
    )


def local(queries, keys, values, out_grad, pair, ln_gain, proj_weight, token_mask, atom_map):
    count = queries.shape[2]
    key_keep = token_mask > 0
    tok_weight = token_weights(atom_map, token_mask)
    wide = pair.astype(jnp.float32)
    center = jnp.mean(wide, axis=-1, keepdims=True)
    spread = jnp.mean(jnp.square(wide - center), axis=-1, keepdims=True)
    inv_std = 1.0 / jnp.sqrt(spread + 1e-05)
    normed = (wide - center) * inv_std
    lnout = (normed * ln_gain).astype(jnp.bfloat16)
    tile_bias = jnp.einsum(
        "ijc,ch->hij", lnout, proj_weight, preferred_element_type=jnp.float32
    ).astype(jnp.bfloat16)
    wide_rows = lax.all_gather(tile_bias, "samp", axis=2, tiled=True)
    bias = lax.all_to_all(wide_rows, "head", split_axis=0, concat_axis=1, tiled=True)

    def one_sample(total, items):
        query_row, key_row, value_row, grad_row = items
        attended, query_grad, key_grad, value_grad, dscore = attend(
            query_row, key_row, value_row, grad_row, bias, key_keep, tok_weight
        )
        return (total + dscore, (attended, query_grad, key_grad, value_grad))

    start = jnp.zeros(bias.shape, jnp.float32)
    bias_partial, outs = lax.scan(one_sample, start, (queries, keys, values, out_grad))
    attended, query_grad, key_grad, value_grad = outs
    summed = lax.psum_scatter(
        bias_partial.astype(jnp.bfloat16), "samp", scatter_dimension=2, tiled=True
    ).astype(jnp.float32)
    bias_grad = lax.all_to_all(
        summed.astype(jnp.bfloat16), "head", split_axis=1, concat_axis=0, tiled=True
    ).astype(summed.dtype)
    highest = lax.Precision.HIGHEST
    lnout_grad = jnp.einsum(
        "hij,ch->ijc", bias_grad, proj_weight.astype(jnp.float32), precision=highest
    )
    weight_part = jnp.einsum("ijc,hij->ch", lnout.astype(jnp.float32), bias_grad, precision=highest)
    gain_part = jnp.sum(lnout_grad * normed, axis=(0, 1))
    weight_sum, gain_sum = lax.psum((weight_part, gain_part), ("samp", "head"))
    scaled = lnout_grad * ln_gain
    pair_grad = (
        scaled
        - jnp.mean(scaled, axis=-1, keepdims=True)
        - normed * jnp.mean(scaled * normed, axis=-1, keepdims=True)
    ) * inv_std
    return (
        attended,
        query_grad,
        key_grad,
        value_grad,
        pair_grad.astype(jnp.bfloat16),
        weight_sum / count,
        gain_sum / count,
    )


def solution(mesh):
    placed = (
        P("samp", "head", None),
        P("samp", "head", None),
        P("samp", "head", None),
        P("samp", "head", None),
        P("head", "samp", None),
        P(),
        P(),
        P(),
        P(),
    )
    return jax.shard_map(
        local,
        mesh=mesh,
        in_specs=placed,
        out_specs=(
            P("samp", "head", None),
            P("samp", "head", None),
            P("samp", "head", None),
            P("samp", "head", None),
            P("head", "samp", None),
            P(),
            P(),
        ),
        check_vma=False,
    )
```

profile of v0, /device:TPU:1, one launch (start us, length us, event | category | flops | bytes accessed | tf_op | source)
XLA Modules:
  0.0 939.2 jit_solution(5410960035745740067)
XLA Ops:
  7.2 0.0 copy-start
  7.2 1.1 convert_reduce_fusion
  8.3 1.1 fusion.25
  9.4 1.2 fusion.4
  10.7 0.0 copy-start.1
  10.7 104.2 %all_gather.3 = bf16[16,32,512]{0,2,1:T(8,128)(2,1)} all-gather(bf16[16,32,16]{0,2,1:T(8,128)(2,1)S(1)} %fusion.4), channel_id=1, replica_groups=mesh['samp'=32,'head'=16] {'samp'}, dimensions={2}, use_global_device_ids=true | all-gather | bytes 540672 | tf_op jit(solution)/shard_map/all_gather | solution.py:74
  114.9 4.6 copy.27
  119.5 17.6 %all-to-all-start = ((bf16[16,32,512]{2,1,0:T(8,128)(2,1)}), bf16[16,32,512]{2,1,0:T(8,128)(2,1)S(1)}, u32[]{:S(2)}, u32[]{:S(2)}) async-start(bf16[16,32,512]{2,1,0:T(8,128)(2,1)} %copy.27), calls=%async_computation | async-start | bytes 1048576 | tf_op jit(solution)/shard_map/all_to_all | solution.py:75
  137.1 0.0 reduce-scatter.2.cloned.1.call-start
  137.1 0.0 copy-done.1
  137.2 0.0 copy-start.5
  137.2 0.0 copy-start.4
  137.2 42.1 %while.32 = (s32[]{:T(128)}, u32[512]{0:T(512)S(1)}, u32[512]{0:T(512)S(1)}, s32[4096]{0:T(1024)S(1)}, s32[]{:T(128)}, /*index=5*/s32[]{:T(128)}, s32[]{}) while((s32[]{:T(128)}, u32[512]{0:T(512)S(1)}, u32[512]{0:T(512)S(1)}, s32[4096]{0:T(1024)S(1)}, s32[]{:T(128)}, /*index=5*/s32[]{:T(128)}, s32[]{}) %tuple.50), condition=%wide.region_5.6_spmd.clone, body=%wide.region_4.5_spmd.clone.sunk | while | flops 10244 | bytes 37989 | solution.py:9
  137.2 3.1 gather_fusion
  140.5 3.1 gather_fusion
  143.7 3.1 gather_fusion
  146.9 3.1 gather_fusion
  150.2 3.1 gather_fusion
  153.4 3.1 gather_fusion
  156.6 3.1 gather_fusion
  159.9 3.1 gather_fusion
  163.1 3.1 gather_fusion
  166.4 3.1 gather_fusion
  169.6 3.1 gather_fusion
  172.8 3.1 gather_fusion
  176.1 3.1 gather_fusion
  179.3 0.0 copy-start.7
  179.3 0.0 copy-start.8
  179.3 0.0 copy-done.5
  179.3 0.1 fusion.51
  179.4 0.0 all-to-all-done
  179.4 0.1 bitcast_convert_fusion
  179.6 0.3 copy.28
  179.9 0.0 copy-done
  179.9 0.0 copy-done.4
  179.9 0.4 fusion.54
  180.3 0.2 fusion.12
  180.5 0.0 copy-done.7
  180.5 0.0 copy-done.8
  180.5 0.4 multiply_reduce_fusion
  180.9 1.1 multiply_convert_fusion
  182.0 0.0 reduce-scatter.2.cloned.1.call-update
  182.0 1.9 fusion.7
  183.9 0.9 fusion.10
  184.8 0.9 fusion.9
  185.7 616.3 %reduce-scatter.2.cloned.1.call-done = bf16[1,512,16]{1,2,0:T(8,128)(2,1)} async-done(((bf16[1,512,512]{1,2,0:T(8,128)(2,1)}), bf16[1,512,16]{1,2,0:T(8,128)(2,1)}) %reduce-scatter.2.cloned.1.call-update) | async-done | bytes 16400 | tf_op jit(solution)/shard_map/reduce_scatter | solution.py:87
  802.0 0.9 copy.29
  802.9 0.5 broadcast.127
  803.4 1.4 reduce.6
  804.9 0.8 reshape.193
  805.6 16.4 %all-to-all-start.1 = ((bf16[16,2,256]{2,1,0:T(2,128)(2,1)}), bf16[16,2,256]{2,1,0:T(2,128)(2,1)S(1)}, u32[]{:S(2)}, u32[]{:S(2)}) async-start(bf16[16,2,256]{2,1,0:T(2,128)(2,1)} %reshape.193), calls=%async_computation.2 | async-start | bytes 32768 | tf_op jit(solution)/shard_map/all_to_all | solution.py:90
  822.0 0.0 copy-done.2
  822.0 0.9 fusion.8
  822.9 4.9 all-to-all-done.1
  827.8 0.2 reshape.194
  828.0 0.1 copy.30
  828.1 0.1 all_to_all.8
  828.2 0.2 copy.32
  828.4 0.4 fusion.24
  828.9 0.3 convolution_bitcast_fusion
  829.2 101.0 %all-reduce = (f32[128,16]{0,1:T(8,128)S(1)}, f32[128]{0:T(128)S(1)}) all-reduce(f32[128,16]{0,1:T(8,128)S(1)} %convolution_bitcast_fusion, f32[128]{0:T(128)S(1)} %get-tuple-element.129), channel_id=1, replica_groups=mesh['samp'=32,'head'=16] {'samp','head'}, use_global_device_ids=true, to_apply=%region_10.11 | all-reduce | flops 2176 | bytes 17408 | tf_op jit(solution)/shard_map/psum | solution.py:99
  930.2 0.6 broadcast_multiply_fusion.3
  930.8 0.5 broadcast_multiply_fusion.4
  931.3 1.0 fusion.23
  (79 shorter events, 0.6 us)
Async XLA Ops:
  7.2 172.8 %copy-start = (bf16[1,48,512]{2,1,0:T(8,128)(2,1)S(1)}, bf16[1,48,512]{2,1,0:T(8,128)(2,1)}, u32[]{:S(2)}) copy-start(bf16[1,48,512]{2,1,0:T(8,128)(2,1)} %param.12) | copy-start | bytes 147460
  10.7 126.5 %copy-start.1 = (s32[4096]{0:T(1024)S(1)}, s32[4096]{0:T(1024)}, u32[]{:S(2)}) copy-start(s32[4096]{0:T(1024)} %param.19) | copy-start | bytes 49156
  119.5 59.9 %all-to-all-start = ((bf16[16,32,512]{2,1,0:T(8,128)(2,1)}), bf16[16,32,512]{2,1,0:T(8,128)(2,1)S(1)}, u32[]{:S(2)}, u32[]{:S(2)}) async-start(bf16[16,32,512]{2,1,0:T(8,128)(2,1)} %copy.27), calls=%async_computation | async-start | bytes 1048576 | tf_op jit(solution)/shard_map/all_to_all | solution.py:75
  137.1 664.9 %reduce-scatter.2.cloned.1.call-start = ((), (), s32[]{:S(2)}) async-start(), calls=%async_computation.3 | async-start | bytes 540672 | tf_op jit(solution)/shard_map/reduce_scatter | solution.py:87
  137.2 42.2 %copy-start.5 = (s32[512]{0:T(512)S(1)}, s32[512]{0:T(512)}, u32[]{:S(2)}) copy-start(s32[512]{0:T(512)} %param.18) | copy-start | bytes 6148
  137.2 42.8 %copy-start.4 = (bf16[1,48,512]{2,1,0:T(8,128)(2,1)S(1)}, bf16[1,48,512]{2,1,0:T(8,128)(2,1)}, u32[]{:S(2)}) copy-start(bf16[1,48,512]{2,1,0:T(8,128)(2,1)} %param.11) | copy-start | bytes 147460
  179.3 1.2 copy-start.7
  179.3 1.2 copy-start.8
  183.9 638.1 %copy-start.2 = (bf16[512,512]{0,1:T(8,128)(2,1)S(1)}, bf16[512,512]{0,1:T(8,128)(2,1)}, u32[]{:S(2)}) copy-start(bf16[512,512]{0,1:T(8,128)(2,1)} %multiply_convert_fusion) | copy-start | bytes 1572868
  184.8 643.6 %copy-start.3 = (bf16[32,16,128]{2,1,0:T(8,128)(2,1)S(1)}, bf16[32,16,128]{2,1,0:T(8,128)(2,1)}, u32[]{:S(2)}) copy-start(bf16[32,16,128]{2,1,0:T(8,128)(2,1)} %param.15) | copy-start | bytes 393220
  184.8 643.6 %copy-start.6 = (f32[128]{0:T(128)S(1)}, f32[128]{0:T(128)}, u32[]{:S(2)}) copy-start(f32[128]{0:T(128)} %param.16) | copy-start | bytes 1540
  184.8 643.6 %copy-start.9 = (bf16[128,16]{0,1:T(8,128)(2,1)S(1)}, bf16[128,16]{0,1:T(8,128)(2,1)}, u32[]{:S(2)}) copy-start(bf16[128,16]{0,1:T(8,128)(2,1)} %param.17) | copy-start | bytes 12292
  805.6 22.2 %all-to-all-start.1 = ((bf16[16,2,256]{2,1,0:T(2,128)(2,1)}), bf16[16,2,256]{2,1,0:T(2,128)(2,1)S(1)}, u32[]{:S(2)}, u32[]{:S(2)}) async-start(bf16[16,2,256]{2,1,0:T(2,128)(2,1)} %reshape.193), calls=%async_computation.2 | async-start | bytes 32768 | tf_op jit(solution)/shard_map/all_to_all | solution.py:90
Sparse Core Ops, SparseCore 0:
  182.1 619.8 reduce-scatter.1
where the time goes:
time: 940 us; the launch traced here: 939 us
  waiting for transfers between devices  621 us (66%)
  blocking collectives  205 us (22%)
  local copies, waits for them, and re-layouts  48.6 us (5%)
  starting transfers between devices  34 us (4%)
  between operations  14.3 us (2%)
    reduce_scatter x1, waiting for transfers between devices, local(): lax.psum_scatter(bias_partial.astype(jnp.bfloat16), 'samp', scatter_dimen...  616 us
    all_gather x1, blocking collectives, local(): wide_rows = lax.all_gather(tile_bias, 'samp', axis=2, tiled=True)  104 us
    psum x1, blocking collectives, local(): weight_sum, gain_sum = lax.psum((weight_part, gain_part), ('samp', 'head'))  101 us
    gather x13, local copies, waits for them, and re-layouts, token_weights(): jnp.searchsorted(atom_map, jnp.arange(count, dtype=jnp.int32), side='right')  40.9 us
  transfers between devices with their start and end apart: 3, of which 2 were waited for; matrix products, arithmetic and copies ran while one was open for 5% of the time, Pallas kernels for 0%

commit v1 on v0

v1 whole, which is shorter than its diff:
```python
import functools
import math

import jax
import jax.numpy as jnp
from jax import lax
from jax.experimental import pallas as pl
from jax.experimental.pallas import tpu as pltpu
from jax.sharding import PartitionSpec as P

MESH = pl.DeviceIdType.MESH
F32 = jnp.float32
BF16 = jnp.bfloat16
LANES = 128
YH = 2


def dot_nn(a, b):
    return lax.dot_general(a, b, (((1,), (0,)), ((), ())), preferred_element_type=F32)


def dot_nt(a, b):
    return lax.dot_general(a, b, (((1,), (1,)), ((), ())), preferred_element_type=F32)


def dot_tn(a, b):
    return lax.dot_general(a, b, (((0,), (0,)), ((), ())), preferred_element_type=F32)


def kernel(
    samp, heads, atoms,
    q_ref, k_ref, v_ref, g_ref, pair_ref, gain_ref, w_ref, mask_ref, atom_ref,
    att_ref, qg_ref, kg_ref, vg_ref, pg_ref, wg_ref, gg_ref,
    xs, norm, inv, ln, tile32, tsend, trecv, bias, score, dprob, probb, dsb, top,
    rin, racc, fin, brecv, part, arr1, row, arr2, tot, res,
    a_send, a_recv, ag_send, ag_recv, rs_send, rs_recv, b_send, b_recv,
    s1, r1, s2, r2, s3, r3,
):
    zn = samp // YH
    hops = zn // 4
    plane = YH * heads
    feat, count = q_ref.shape
    tj, ti = count // samp, count // heads
    groups = LANES // ti
    tiles = count // LANES
    inv_root = 1.0 / math.sqrt(feat)

    me_s, me_h = lax.axis_index("samp"), lax.axis_index("head")
    yh, z = me_s // zn, lax.rem(me_s, zn)
    me_p = yh * heads + me_h
    grp = lax.rem(me_h, groups)

    def at_plane(p):
        return (p // heads) * zn + z, lax.rem(p, heads)

    def wrap(o):
        return lax.rem(z + (o + 2 * zn), zn)

    def at_z(o):
        return yh * zn + wrap(o), me_h

    barrier = pltpu.get_barrier_semaphore()

    def greet(off, c):
        pl.semaphore_signal(barrier, inc=1, device_id=at_plane(lax.rem(me_p + off, plane)), device_id_type=MESH)
        return c

    lax.fori_loop(1, plane, greet, 0)
    for o in (1, -1, 2, -2):
        pl.semaphore_signal(barrier, inc=1, device_id=at_z(o), device_id_type=MESH)

    gain = gain_ref[...]
    xs[...] = pair_ref[...].astype(F32).reshape(ti * tj, LANES)
    for j in range(tj):
        x = xs[pl.ds(j, ti, stride=tj), :]
        mu = jnp.mean(x, axis=-1, keepdims=True)
        d = x - mu
        iv = 1.0 / jnp.sqrt(jnp.mean(d * d, axis=-1, keepdims=True) + 1e-05)
        n = d * iv
        rows = slice(j * ti, (j + 1) * ti)
        norm[rows, :] = n
        inv[rows, :] = jnp.broadcast_to(iv, (ti, LANES))
        ln[rows, :] = (n * gain).astype(BF16)
    wt = w_ref[...]
    zb = dot_nt(wt, ln[...])
    lane_group = lax.broadcasted_iota(jnp.int32, (heads, LANES), 1) // ti
    for j in range(tj):
        t, jj = j // groups, j % groups
        turned = pltpu.roll(zb[:, t * LANES : (t + 1) * LANES], lax.rem(grp - jj + groups, groups) * ti, axis=1)
        tile32[pl.ds(j, heads, stride=tj), :] = jnp.where(lane_group == grp, turned, 0.0)
    tsend[...] = tile32[...].reshape(heads, tj, LANES).astype(BF16)

    pl.semaphore_wait(barrier, plane - 1 + 4)

    def all_of(ref, n, sem):
        return pltpu.make_async_copy(ref.at[pl.ds(0, n)], ref.at[pl.ds(0, n)], sem)

    def plane_send(src_of, dst, send, recv):
        def body(off, c):
            p = lax.rem(me_p + off, plane)
            pltpu.make_async_remote_copy(
                src_ref=src_of(p), dst_ref=dst.at[me_p], send_sem=send, recv_sem=recv,
                device_id=at_plane(p), device_id_type=MESH,
            ).start()
            return c

        lax.fori_loop(1, plane, body, 0)

    plane_send(lambda p: tsend.at[lax.rem(p, heads)], trecv, a_send.at[0], a_recv.at[0])
    trecv[me_p] = tsend[me_h]

    length = jnp.sum(mask_ref[...].astype(F32), axis=(0, 1), keepdims=True)
    step = 64

    def counting(c, carry):
        ids = lax.broadcasted_iota(jnp.int32, (step, LANES), 0) + c * step
        acc = jnp.zeros((step, LANES), F32)
        for r in range(atoms // LANES):
            acc = acc + jnp.where(atom_ref[r : r + 1, :] == ids, 1.0, 0.0)
        xs[pl.ds(pl.multiple_of(c * step, step), step), :] = acc
        return carry

    lax.fori_loop(0, count // step, counting, 0)
    counts = dot_nt(jnp.ones((8, LANES), BF16), xs[0:count, :].astype(BF16))[0:1, :]
    real = lax.broadcasted_iota(jnp.int32, (1, count), 1).astype(F32) < length
    tok = jnp.where(real, counts * (count / atoms), 0.0)
    query, key, value = q_ref[...], k_ref[...], v_ref[...]
    grad = (g_ref[...].astype(F32) * tok).astype(BF16)
    chunk = LANES // tj
    for c in range(tiles):
        cols = slice(c * LANES, (c + 1) * LANES)
        keep = lax.broadcasted_iota(jnp.int32, (LANES, 1), 0).astype(F32) + float(c * LANES) < length
        s = jnp.where(keep, dot_tn(key[:, cols], query) * inv_root, -1000000000.0)
        score[c * chunk : (c + 1) * chunk] = s.reshape(chunk, tj, count)
        dprob[c * chunk : (c + 1) * chunk] = dot_tn(value[:, cols], grad).reshape(chunk, tj, count)
    top[...] = jnp.full(top.shape, -3.0e38, F32)

    all_of(trecv, plane - 1, a_recv.at[0]).wait()
    for y in range(YH):
        for t in range(tiles):
            block = trecv[y * heads + t * groups]
            for u in range(1, groups):
                block = block + trecv[y * heads + t * groups + u]
            bias[y, z, :, t * LANES : (t + 1) * LANES] = block

    def ag_copy(sem, origin, o):
        return pltpu.make_async_remote_copy(
            src_ref=bias.at[:, wrap(origin)], dst_ref=bias.at[:, wrap(origin)],
            send_sem=ag_send.at[sem], recv_sem=ag_recv.at[sem], device_id=at_z(o), device_id_type=MESH,
        )

    def absorb(origin):
        o = wrap(origin)
        best = top[...]
        for y in range(YH):
            s = score[y * zn + o] + bias[y, o].astype(F32)
            score[y * zn + o] = s
            best = jnp.maximum(best, jnp.max(s.reshape(tj // 8, 8, count), axis=0))
        top[...] = best

    def up2(t): return ag_copy(4 * t, -2 * t, 2)
    def up1(t): return ag_copy(4 * t + 1, -2 * t, 1)
    def dn2(t): return ag_copy(4 * t + 2, 2 * t, -2)
    def dn1(t): return ag_copy(4 * t + 3, 2 * t, -1)

    sent = []

    def go(copy):
        copy.start()
        sent.append(copy)

    for t in range(hops):
        if t:
            up2(t - 1).wait_recv()
        go(up2(t))
        go(up1(t))
        if t:
            dn2(t - 1).wait_recv()
        if t < hops - 1:
            go(dn2(t))
        go(dn1(t))
        if t == 0:
            absorb(0)
        else:
            absorb(-2 * t)
            absorb(2 * t)
            up1(t - 1).wait_recv()
            absorb(-2 * t + 1)
            dn1(t - 1).wait_recv()
            absorb(2 * t - 1)
    up1(hops - 1).wait_recv()
    absorb(-2 * hops + 1)
    dn1(hops - 1).wait_recv()
    absorb(2 * hops - 1)
    up2(hops - 1).wait_recv()
    absorb(-2 * hops)

    largest = jnp.max(top[...], axis=0, keepdims=True)

    def first(b, carry):
        total, dots = carry
        p = jnp.exp(score[pl.ds(b * 2, 2)] - largest[None])
        score[pl.ds(b * 2, 2)] = p
        pd = p * dprob[pl.ds(b * 2, 2)]
        return (
            total + jnp.sum(p.reshape(2 * tj // 8, 8, count), axis=0),
            dots + jnp.sum(pd.reshape(2 * tj // 8, 8, count), axis=0),
        )

    zero = jnp.zeros((8, count), F32)
    total, dots = lax.fori_loop(0, samp // 2, first, (zero, zero))
    scale = 1.0 / jnp.sum(total, axis=0, keepdims=True)
    row_dot = jnp.sum(dots, axis=0, keepdims=True) * scale

    def second(b, carry):
        for y in range(YH):
            prob = score[y * zn + b] * scale
            probb[y, b] = prob.astype(BF16)
            dsb[y, b] = (prob * (dprob[y * zn + b] - row_dot)).astype(BF16)
        return carry

    lax.fori_loop(0, zn, second, 0)

    def rs_copy(sem, src, o):
        return pltpu.make_async_remote_copy(
            src_ref=src, dst_ref=rin.at[sem], send_sem=rs_send.at[sem], recv_sem=rs_recv.at[sem],
            device_id=at_z(o), device_id_type=MESH,
        )

    def own(o):
        return dsb.at[:, wrap(o)]

    def arrived(sem):
        rs_copy(sem, own(0), 1).wait_recv()
        return rin[sem].astype(F32)

    def one_matmul(k):
        p2 = probb[...].reshape(count, count) if k in (0, 3) else None
        d2 = dsb[...].reshape(count, count) if k in (1, 2) else None
        if k == 0:
            att_ref[...] = dot_nn(value, p2).astype(BF16)
        elif k == 1:
            qg_ref[...] = (dot_nn(key, d2) * inv_root).astype(BF16)
        elif k == 2:
            kg_ref[...] = (dot_nt(query, d2) * inv_root).astype(BF16)
        else:
            vg_ref[...] = dot_nt(grad, p2).astype(BF16)

    far = 2 * hops
    for t in range(hops):
        if t == 0:
            go(rs_copy(2, own(-far), -2))
        else:
            racc[2 * t] = (dsb[:, wrap(2 * t - far)].astype(F32) + arrived(4 * t - 2) + arrived(4 * t - 1)).astype(BF16)
            go(rs_copy(4 * t + 2, racc.at[2 * t], -2))
            acc = dsb[:, wrap(far - 2 * t)].astype(F32) + arrived(4 * t - 3)
            if t > 1:
                acc = acc + arrived(4 * t - 4)
            racc[2 * t + 1] = acc.astype(BF16)
            go(rs_copy(4 * t, racc.at[2 * t + 1], 2))
        go(rs_copy(4 * t + 3, own(2 * t + 1 - far), -1))
        go(rs_copy(4 * t + 1, own(far - 2 * t - 1), 1))
        for m in range(t * 4 // hops, (t + 1) * 4 // hops):
            one_matmul(m)
    last = 4 * hops
    acc = dsb[:, z].astype(F32) + arrived(last - 3) + arrived(last - 1) + arrived(last - 2)
    if hops > 1:
        acc = acc + arrived(last - 4)
    for t in range(tiles):
        fin[:, t] = acc[:, :, t * LANES : (t + 1) * LANES].astype(BF16)

    plane_send(lambda p: fin.at[p // heads, lax.rem(p, heads) // groups], brecv, b_send.at[0], b_recv.at[0])
    brecv[me_p] = fin[yh, me_h // groups]
    all_of(brecv, plane - 1, b_recv.at[0]).wait()
    tile32[...] = (brecv[0:heads].astype(F32) + brecv[heads:].astype(F32)).reshape(heads * tj, LANES)
    pieces = []
    for t in range(tj // groups):
        piece = jnp.zeros((heads, LANES), F32)
        for jj in range(groups):
            r = tile32[pl.ds(t * groups + jj, heads, stride=tj), :]
            turned = pltpu.roll(r, lax.rem(jj - grp + groups, groups) * ti, axis=1)
            piece = jnp.where(lane_group == jj, turned, piece)
        pieces.append(piece)
    bg = jnp.concatenate(pieces, axis=1)
    hi = bg.astype(BF16)
    lo = (bg - hi.astype(F32)).astype(BF16)
    wpart = dot_nn(hi, ln[...]) + dot_nn(lo, ln[...])
    lng = dot_tn(hi, wt) + dot_tn(lo, wt)
    for r in range(heads):
        part[r] = wpart[r : r + 1, :]
    part[heads] = jnp.sum(lng * norm[...], axis=0, keepdims=True)
    for r in range(heads + 1, plane):
        part[r] = jnp.zeros((1, LANES), F32)

    plane_send(lambda p: part.at[p], arr1, s1.at[0], r1.at[0])
    arr1[me_p] = part[me_p]

    for j in range(tj):
        rows = slice(j * ti, (j + 1) * ti)
        n = norm[rows, :]
        dn = lng[rows, :] * gain
        out = dn - jnp.mean(dn, axis=-1, keepdims=True) - n * jnp.mean(dn * n, axis=-1, keepdims=True)
        xs[pl.ds(j, ti, stride=tj), :] = out * inv[rows, :]
    pg_ref[...] = xs[...].reshape(ti, tj, LANES).astype(BF16)

    all_of(arr1, plane - 1, r1.at[0]).wait()
    row[...] = jnp.sum(arr1[...], axis=0)

    def z_send(off, c):
        pltpu.make_async_remote_copy(
            src_ref=row, dst_ref=arr2.at[z], send_sem=s2.at[0], recv_sem=r2.at[0],
            device_id=at_z(off), device_id_type=MESH,
        ).start()
        return c

    lax.fori_loop(1, zn, z_send, 0)
    arr2[z] = row[...]
    all_of(arr2, zn - 1, r2.at[0]).wait()
    tot[...] = jnp.sum(arr2[...], axis=0) * (1.0 / count)
    plane_send(lambda p: tot, res, s3.at[0], r3.at[0])
    res[me_p] = tot[...]
    all_of(res, plane - 1, r3.at[0]).wait()
    wg_ref[...] = jnp.concatenate([res[r] for r in range(heads)], axis=0)
    gg_ref[...] = res[heads]

    all_of(trecv, plane - 1, a_send.at[0]).wait()
    for copy in sent:
        copy.wait_send()
    all_of(brecv, plane - 1, b_send.at[0]).wait()
    all_of(arr1, plane - 1, s1.at[0]).wait()
    all_of(arr2, zn - 1, s2.at[0]).wait()
    all_of(res, plane - 1, s3.at[0]).wait()


def local(samp, heads, queries, keys, values, out_grad, pair, ln_gain, proj_weight, token_mask, atom_map):
    _, feat, count = queries.shape
    ti, tj, chan = pair.shape
    atoms = atom_map.shape[0]
    zn = samp // YH
    hops = zn // 4
    plane = YH * heads
    tiles = count // LANES
    vmem = pl.BlockSpec(memory_space=pltpu.VMEM)
    row = (1, LANES)
    dma = pltpu.SemaphoreType.DMA
    scratch = [
        pltpu.VMEM((max(ti * tj, count), LANES), F32),
        pltpu.VMEM((ti * tj, LANES), F32),
        pltpu.VMEM((ti * tj, LANES), F32),
        pltpu.VMEM((ti * tj, LANES), BF16),
        pltpu.VMEM((heads * tj, LANES), F32),
        pltpu.VMEM((heads, tj, LANES), BF16),
        pltpu.VMEM((plane, tj, LANES), BF16),
        pltpu.VMEM((YH, zn, tj, count), BF16),
        pltpu.VMEM((samp, tj, count), F32),
        pltpu.VMEM((samp, tj, count), F32),
        pltpu.VMEM((YH, zn, tj, count), BF16),
        pltpu.VMEM((YH, zn, tj, count), BF16),
        pltpu.VMEM((8, count), F32),
        pltpu.VMEM((4 * hops, YH, tj, count), BF16),
        pltpu.VMEM((2 * hops, YH, tj, count), BF16),
        pltpu.VMEM((YH, tiles, tj, LANES), BF16),
        pltpu.VMEM((plane, tj, LANES), BF16),
        pltpu.VMEM((plane,) + row, F32),
        pltpu.VMEM((plane,) + row, F32),
        pltpu.VMEM(row, F32),
        pltpu.VMEM((zn,) + row, F32),
        pltpu.VMEM(row, F32),
        pltpu.VMEM((plane,) + row, F32),
        dma((1,)), dma((1,)), dma((4 * hops,)), dma((4 * hops,)), dma((4 * hops,)), dma((4 * hops,)),
        dma((1,)), dma((1,)), dma((1,)), dma((1,)), dma((1,)), dma((1,)), dma((1,)), dma((1,)),
    ]
    shape = jax.ShapeDtypeStruct
    att, qg, kg, vg, pg, wg, gg = pl.pallas_call(
        functools.partial(kernel, samp, heads, atoms),
        out_shape=(
            shape((feat, count), BF16), shape((feat, count), BF16), shape((feat, count), BF16),
            shape((feat, count), BF16), shape((ti, tj, chan), BF16), shape((heads, chan), F32), shape((1, chan), F32),
        ),
        in_specs=[vmem] * 9,
        out_specs=(vmem,) * 7,
        scratch_shapes=scratch,
        compiler_params=pltpu.CompilerParams(
            collective_id=0, has_side_effects=True, vmem_limit_bytes=48 * 1024 * 1024
        ),
    )(
        queries[0], keys[0], values[0], out_grad[0], pair, ln_gain.reshape(1, chan), proj_weight.T,
        token_mask.reshape(tiles, LANES), atom_map.reshape(atoms // LANES, LANES),
    )
    return att[None], qg[None], kg[None], vg[None], pg, wg.T, gg[0]


def solution(mesh):
    cut = P("samp", "head", None)
    return jax.shard_map(
        functools.partial(local, mesh.shape["samp"], mesh.shape["head"]),
        mesh=mesh,
        in_specs=(cut, cut, cut, cut, P("head", "samp", None), P(), P(), P(), P()),
        out_specs=(cut, cut, cut, cut, P("head", "samp", None), P(), P()),
        check_vma=False,
    )
```

time: 940 us -> 88.3 us (0.09)
  waiting for transfers between devices: 621 us -> 0 us
  blocking collectives: 205 us -> 0 us
  Pallas kernels: 0 us -> 77.4 us
  local copies, waits for them, and re-layouts: 48.6 us -> 9.73 us
  starting transfers between devices: 34 us -> 0 us
  between operations: 14.3 us -> 0.68 us
    reduce_scatter x1 -> x0, waiting for transfers between devices: 616 us -> none  [local(): lax.psum_scatter(bias_partial.astype(jnp.bfloat16), 'samp', scatter_dimen...]
    all_gather x1 -> x0, blocking collectives: 104 us -> none  [local(): wide_rows = lax.all_gather(tile_bias, 'samp', axis=2, tiled=True)]
    psum x1 -> x0, blocking collectives: 101 us -> none  [local(): weight_sum, gain_sum = lax.psum((weight_part, gain_part), ('samp', 'head'))]
    pallas_call x0 -> x1, Pallas kernels: none -> 77.4 us  [local(): pl.pallas_call(functools.partial(kernel, samp, heads, atoms), out_shape=(...]
    gather x13 -> x0, local copies, waits for them, and re-layouts: 40.9 us -> none  [token_weights(): jnp.searchsorted(atom_map, jnp.arange(count, dtype=jnp.int32), side='right')]
    all_to_all x2 -> x0, starting transfers between devices: 33.9 us -> none  [the longest x1 17.6 us: local(): lax.all_to_all(wide_rows, 'head', split_axis=0, concat_axis=1, tiled=True)]
  transfers between devices with their start and end apart: 3 -> 0, of which waited for: 2 -> 0; matrix products, arithmetic and copies ran while one was open for 5% -> 0% of each run, Pallas kernels for 0% -> 0%
where the time goes in v1:
time: 88.3 us; the launch traced here: 87.8 us
  Pallas kernels  77.4 us (88%)
  local copies, waits for them, and re-layouts  9.73 us (11%)
    pallas_call x1, Pallas kernels, local(): pl.pallas_call(functools.partial(kernel, samp, heads, atoms), out_shape=(...  77.4 us
    unnamed x25, local copies, waits for them, and re-layouts  9.73 us

profile of v1, /device:TPU:1, one launch (start us, length us, event | category | flops | bytes accessed | tf_op | source)
XLA Modules:
  0.0 87.8 jit_solution(15962267697977866164)
XLA Ops:
  0.6 0.0 copy-start.6
  0.6 0.0 copy-start.7
  0.7 0.0 copy-start.8
  0.7 0.7 copy-done.6
  1.3 0.0 copy-done.7
  1.3 0.0 copy-done.8
  1.3 0.0 copy-start
  1.3 0.9 %copy-done = bf16[32,16,128]{2,1,0:T(8,128)(2,1)S(1)} copy-done((bf16[32,16,128]{2,1,0:T(8,128)(2,1)S(1)}, bf16[32,16,128]{2,1,0:T(8,128)(2,1)}, u32[]{:S(2)}) %copy-start) | copy-done | bytes 131096
  2.2 0.0 copy-start.1
  2.2 0.8 copy-done.1
  3.0 0.0 copy-start.2
  3.0 0.8 copy-done.2
  3.8 0.0 copy-start.3
  3.8 0.8 copy-done.3
  4.6 0.0 copy-start.4
  4.6 0.8 copy-done.4
  5.4 0.0 copy-start.5
  5.4 0.7 copy-done.5
  6.2 77.4 %shard_map.144 = (bf16[48,512]{1,0:T(8,128)(2,1)S(1)}, bf16[48,512]{1,0:T(8,128)(2,1)S(1)}, bf16[48,512]{1,0:T(8,128)(2,1)S(1)}, bf16[48,512]{1,0:T(8,128)(2,1)S...) custom-call(bf16[48,512]{1,0:T(8,128)(2,1)S(1)} %bitcast.18, ...), custom_call_target="tpu_custom_call" | custom-call | tf_op jit(solution)/shard_map/pallas_call | solution.py:374
  83.6 0.6 copy.23
  84.2 0.6 copy.24
  84.8 0.6 copy.25
  85.4 0.6 copy.26
  86.1 0.7 copy.27
  86.7 0.6 copy.28
  87.3 0.5 copy.29
Async XLA Ops:
  0.6 0.7 copy-start.6
  0.6 0.7 copy-start.7
  0.7 0.7 copy-start.8
  1.3 0.9 %copy-start = (bf16[32,16,128]{2,1,0:T(8,128)(2,1)S(1)}, bf16[32,16,128]{2,1,0:T(8,128)(2,1)}, u32[]{:S(2)}) copy-start(bf16[32,16,128]{2,1,0:T(8,128)(2,1)} %pair_ref.1) | copy-start | bytes 393220
  2.2 0.8 copy-start.1
  3.0 0.8 copy-start.2
  3.8 0.8 copy-start.3
  4.6 0.8 copy-start.4
  5.4 0.7 copy-start.5

commit v2 on v1

--- a/solution.py
+++ b/solution.py
@@ -29,13 +29,21 @@
 
 def kernel(
     samp, heads, atoms,
-    q_ref, k_ref, v_ref, g_ref, pair_ref, gain_ref, w_ref, mask_ref, atom_ref,
+    pair_hbm, gain_hbm, w_hbm, mask_hbm, atom_hbm, g_hbm, q_hbm, k_hbm, v_hbm,
     att_ref, qg_ref, kg_ref, vg_ref, pg_ref, wg_ref, gg_ref,
+    pair_ref, gain_ref, w_ref, mask_ref, atom_ref, g_ref, q_ref, k_ref, v_ref,
     xs, norm, inv, ln, tile32, tsend, trecv, bias, score, dprob, probb, dsb, top,
     rin, racc, fin, brecv, part, arr1, row, arr2, tot, res,
     a_send, a_recv, ag_send, ag_recv, rs_send, rs_recv, b_send, b_recv,
-    s1, r1, s2, r2, s3, r3,
+    s1, r1, s2, r2, s3, r3, in_sem,
 ):
+    arrays = (
+        (pair_hbm, pair_ref), (gain_hbm, gain_ref), (w_hbm, w_ref), (mask_hbm, mask_ref), (atom_hbm, atom_ref),
+        (g_hbm, g_ref), (q_hbm, q_ref), (k_hbm, k_ref), (v_hbm, v_ref),
+    )
+    loads = [pltpu.make_async_copy(src, dst, in_sem.at[i]) for i, (src, dst) in enumerate(arrays)]
+    for load in loads:
+        load.start()
     zn = samp // YH
     hops = zn // 4
     plane = YH * heads
@@ -65,9 +73,12 @@
         pl.semaphore_signal(barrier, inc=1, device_id=at_plane(lax.rem(me_p + off, plane)), device_id_type=MESH)
         return c
 
-    lax.fori_loop(1, plane, greet, 0)
+    lax.fori_loop(1, plane, greet, 0, unroll=True)
     for o in (1, -1, 2, -2):
         pl.semaphore_signal(barrier, inc=1, device_id=at_z(o), device_id_type=MESH)
+
+    for load in loads[:3]:
+        load.wait()
 
     gain = gain_ref[...]
     xs[...] = pair_ref[...].astype(F32).reshape(ti * tj, LANES)
@@ -104,11 +115,13 @@
             ).start()
             return c
 
-        lax.fori_loop(1, plane, body, 0)
+        lax.fori_loop(1, plane, body, 0, unroll=True)
 
     plane_send(lambda p: tsend.at[lax.rem(p, heads)], trecv, a_send.at[0], a_recv.at[0])
     trecv[me_p] = tsend[me_h]
 
+    for load in loads[3:]:
+        load.wait()
     length = jnp.sum(mask_ref[...].astype(F32), axis=(0, 1), keepdims=True)
     step = 64
 
@@ -127,13 +140,19 @@
     query, key, value = q_ref[...], k_ref[...], v_ref[...]
     grad = (g_ref[...].astype(F32) * tok).astype(BF16)
     chunk = LANES // tj
-    for c in range(tiles):
-        cols = slice(c * LANES, (c + 1) * LANES)
-        keep = lax.broadcasted_iota(jnp.int32, (LANES, 1), 0).astype(F32) + float(c * LANES) < length
-        s = jnp.where(keep, dot_tn(key[:, cols], query) * inv_root, -1000000000.0)
-        score[c * chunk : (c + 1) * chunk] = s.reshape(chunk, tj, count)
-        dprob[c * chunk : (c + 1) * chunk] = dot_tn(value[:, cols], grad).reshape(chunk, tj, count)
     top[...] = jnp.full(top.shape, -3.0e38, F32)
+
+    def raw_scores():
+        for c in range(tiles):
+            cols = slice(c * LANES, (c + 1) * LANES)
+            keep = lax.broadcasted_iota(jnp.int32, (LANES, 1), 0).astype(F32) + float(c * LANES) < length
+            s = jnp.where(keep, dot_tn(key[:, cols], query) * inv_root, -1000000000.0)
+            score[c * chunk : (c + 1) * chunk] = s.reshape(chunk, tj, count)
+
+    def raw_dprob():
+        for c in range(tiles):
+            cols = slice(c * LANES, (c + 1) * LANES)
+            dprob[c * chunk : (c + 1) * chunk] = dot_tn(value[:, cols], grad).reshape(chunk, tj, count)
 
     all_of(trecv, plane - 1, a_recv.at[0]).wait()
     for y in range(YH):
@@ -143,10 +162,10 @@
                 block = block + trecv[y * heads + t * groups + u]
             bias[y, z, :, t * LANES : (t + 1) * LANES] = block
 
-    def ag_copy(sem, origin, o):
+    def ag_copy(sem, y, origin, o):
         return pltpu.make_async_remote_copy(
-            src_ref=bias.at[:, wrap(origin)], dst_ref=bias.at[:, wrap(origin)],
-            send_sem=ag_send.at[sem], recv_sem=ag_recv.at[sem], device_id=at_z(o), device_id_type=MESH,
+            src_ref=bias.at[y, wrap(origin)], dst_ref=bias.at[y, wrap(origin)],
+            send_sem=ag_send.at[y, sem], recv_sem=ag_recv.at[y, sem], device_id=at_z(o), device_id_type=MESH,
         )
 
     def absorb(origin):
@@ -158,10 +177,10 @@
             best = jnp.maximum(best, jnp.max(s.reshape(tj // 8, 8, count), axis=0))
         top[...] = best
 
-    def up2(t): return ag_copy(4 * t, -2 * t, 2)
-    def up1(t): return ag_copy(4 * t + 1, -2 * t, 1)
-    def dn2(t): return ag_copy(4 * t + 2, 2 * t, -2)
-    def dn1(t): return ag_copy(4 * t + 3, 2 * t, -1)
+    def up2(t, y): return ag_copy(4 * t, y, -2 * t, 2)
+    def up1(t, y): return ag_copy(4 * t + 1, y, -2 * t, 1)
+    def dn2(t, y): return ag_copy(4 * t + 2, y, 2 * t, -2)
+    def dn1(t, y): return ag_copy(4 * t + 3, y, 2 * t, -1)
 
     sent = []
 
@@ -169,30 +188,41 @@
         copy.start()
         sent.append(copy)
 
+    both = range(YH)
     for t in range(hops):
-        if t:
-            up2(t - 1).wait_recv()
-        go(up2(t))
-        go(up1(t))
-        if t:
-            dn2(t - 1).wait_recv()
-        if t < hops - 1:
-            go(dn2(t))
-        go(dn1(t))
+        for y in both:
+            if t:
+                up2(t - 1, y).wait_recv()
+            go(up2(t, y))
+            if t:
+                dn2(t - 1, y).wait_recv()
+            if t < hops - 1:
+                go(dn2(t, y))
+        for y in both:
+            go(up1(t, y))
+            go(dn1(t, y))
         if t == 0:
+            raw_scores()
             absorb(0)
         else:
+            if t == 1:
+                raw_dprob()
             absorb(-2 * t)
             absorb(2 * t)
-            up1(t - 1).wait_recv()
+            for y in both:
+                up1(t - 1, y).wait_recv()
+                dn1(t - 1, y).wait_recv()
             absorb(-2 * t + 1)
-            dn1(t - 1).wait_recv()
             absorb(2 * t - 1)
-    up1(hops - 1).wait_recv()
+    if hops == 1:
+        raw_dprob()
+    for y in both:
+        up1(hops - 1, y).wait_recv()
+        dn1(hops - 1, y).wait_recv()
     absorb(-2 * hops + 1)
-    dn1(hops - 1).wait_recv()
     absorb(2 * hops - 1)
-    up2(hops - 1).wait_recv()
+    for y in both:
+        up2(hops - 1, y).wait_recv()
     absorb(-2 * hops)
 
     largest = jnp.max(top[...], axis=0, keepdims=True)
@@ -221,18 +251,21 @@
 
     lax.fori_loop(0, zn, second, 0)
 
-    def rs_copy(sem, src, o):
+    def rs_copy(sem, y, src, o):
         return pltpu.make_async_remote_copy(
-            src_ref=src, dst_ref=rin.at[sem], send_sem=rs_send.at[sem], recv_sem=rs_recv.at[sem],
+            src_ref=src, dst_ref=rin.at[sem, y], send_sem=rs_send.at[y, sem], recv_sem=rs_recv.at[y, sem],
             device_id=at_z(o), device_id_type=MESH,
         )
 
-    def own(o):
-        return dsb.at[:, wrap(o)]
-
-    def arrived(sem):
-        rs_copy(sem, own(0), 1).wait_recv()
-        return rin[sem].astype(F32)
+    def own(o, y):
+        return dsb.at[y, wrap(o)]
+
+    def mine(o, y):
+        return dsb[y, wrap(o)].astype(F32)
+
+    def arrived(sem, y):
+        rs_copy(sem, y, own(0, y), 1).wait_recv()
+        return rin[sem, y].astype(F32)
 
     def one_matmul(k):
         p2 = probb[...].reshape(count, count) if k in (0, 3) else None
@@ -247,27 +280,39 @@
             vg_ref[...] = dot_nt(grad, p2).astype(BF16)
 
     far = 2 * hops
+
+    def near(t):
+        for y in both:
+            go(rs_copy(4 * t + 3, y, own(2 * t + 1 - far, y), -1))
+            go(rs_copy(4 * t + 1, y, own(far - 2 * t - 1, y), 1))
+
     for t in range(hops):
+        for y in both:
+            if t == 0:
+                go(rs_copy(2, y, own(-far, y), -2))
+            else:
+                racc[2 * t, y] = (
+                    mine(2 * t - far, y) + arrived(4 * t - 2, y) + arrived(4 * t - 1, y)
+                ).astype(BF16)
+                go(rs_copy(4 * t + 2, y, racc.at[2 * t, y], -2))
+                acc = mine(far - 2 * t, y) + arrived(4 * t - 3, y)
+                if t > 1:
+                    acc = acc + arrived(4 * t - 4, y)
+                racc[2 * t + 1, y] = acc.astype(BF16)
+                go(rs_copy(4 * t, y, racc.at[2 * t + 1, y], 2))
         if t == 0:
-            go(rs_copy(2, own(-far), -2))
-        else:
-            racc[2 * t] = (dsb[:, wrap(2 * t - far)].astype(F32) + arrived(4 * t - 2) + arrived(4 * t - 1)).astype(BF16)
-            go(rs_copy(4 * t + 2, racc.at[2 * t], -2))
-            acc = dsb[:, wrap(far - 2 * t)].astype(F32) + arrived(4 * t - 3)
-            if t > 1:
-                acc = acc + arrived(4 * t - 4)
-            racc[2 * t + 1] = acc.astype(BF16)
-            go(rs_copy(4 * t, racc.at[2 * t + 1], 2))
-        go(rs_copy(4 * t + 3, own(2 * t + 1 - far), -1))
-        go(rs_copy(4 * t + 1, own(far - 2 * t - 1), 1))
+            near(0)
+        if t < hops - 1:
+            near(t + 1)
         for m in range(t * 4 // hops, (t + 1) * 4 // hops):
             one_matmul(m)
     last = 4 * hops
-    acc = dsb[:, z].astype(F32) + arrived(last - 3) + arrived(last - 1) + arrived(last - 2)
-    if hops > 1:
-        acc = acc + arrived(last - 4)
-    for t in range(tiles):
-        fin[:, t] = acc[:, :, t * LANES : (t + 1) * LANES].astype(BF16)
+    for y in both:
+        acc = mine(0, y) + arrived(last - 3, y) + arrived(last - 1, y) + arrived(last - 2, y)
+        if hops > 1:
+            acc = acc + arrived(last - 4, y)
+        for t in range(tiles):
+            fin[y, t] = acc[:, t * LANES : (t + 1) * LANES].astype(BF16)
 
     plane_send(lambda p: fin.at[p // heads, lax.rem(p, heads) // groups], brecv, b_send.at[0], b_recv.at[0])
     brecv[me_p] = fin[yh, me_h // groups]
@@ -313,7 +358,7 @@
         ).start()
         return c
 
-    lax.fori_loop(1, zn, z_send, 0)
+    lax.fori_loop(1, zn, z_send, 0, unroll=True)
     arr2[z] = row[...]
     all_of(arr2, zn - 1, r2.at[0]).wait()
     tot[...] = jnp.sum(arr2[...], axis=0) * (1.0 / count)
@@ -330,6 +375,15 @@
     all_of(arr1, plane - 1, s1.at[0]).wait()
     all_of(arr2, zn - 1, s2.at[0]).wait()
     all_of(res, plane - 1, s3.at[0]).wait()
+
+
+def put_out(*refs):
+    sem = refs[-1]
+    copies = [pltpu.make_async_copy(refs[i], refs[7 + i], sem.at[i]) for i in range(7)]
+    for copy in copies:
+        copy.start()
+    for copy in copies:
+        copy.wait()
 
 
 def local(samp, heads, queries, keys, values, out_grad, pair, ln_gain, proj_weight, token_mask, atom_map):
@@ -343,7 +397,11 @@
     vmem = pl.BlockSpec(memory_space=pltpu.VMEM)
     row = (1, LANES)
     dma = pltpu.SemaphoreType.DMA
-    scratch = [
+    operands = (
+        pair, ln_gain.reshape(1, chan), proj_weight.T, token_mask.reshape(tiles, LANES),
+        atom_map.reshape(atoms // LANES, LANES), out_grad[0], queries[0], keys[0], values[0],
+    )
+    scratch = [pltpu.VMEM(x.shape, x.dtype) for x in operands] + [
         pltpu.VMEM((max(ti * tj, count), LANES), F32),
         pltpu.VMEM((ti * tj, LANES), F32),
         pltpu.VMEM((ti * tj, LANES), F32),
@@ -367,26 +425,33 @@
         pltpu.VMEM((zn,) + row, F32),
         pltpu.VMEM(row, F32),
         pltpu.VMEM((plane,) + row, F32),
-        dma((1,)), dma((1,)), dma((4 * hops,)), dma((4 * hops,)), dma((4 * hops,)), dma((4 * hops,)),
-        dma((1,)), dma((1,)), dma((1,)), dma((1,)), dma((1,)), dma((1,)), dma((1,)), dma((1,)),
+        dma((1,)), dma((1,)), dma((YH, 4 * hops)), dma((YH, 4 * hops)), dma((YH, 4 * hops)), dma((YH, 4 * hops)),
+        dma((1,)), dma((1,)), dma((1,)), dma((1,)), dma((1,)), dma((1,)), dma((1,)), dma((1,)), dma((9,)),
     ]
     shape = jax.ShapeDtypeStruct
-    att, qg, kg, vg, pg, wg, gg = pl.pallas_call(
+    outs = (
+        shape((feat, count), BF16), shape((feat, count), BF16), shape((feat, count), BF16),
+        shape((feat, count), BF16), shape((ti, tj, chan), BF16), shape((heads, chan), F32), shape((1, chan), F32),
+    )
+    hbm = pl.BlockSpec(memory_space=pltpu.HBM)
+    results = pl.pallas_call(
         functools.partial(kernel, samp, heads, atoms),
-        out_shape=(
-            shape((feat, count), BF16), shape((feat, count), BF16), shape((feat, count), BF16),
-            shape((feat, count), BF16), shape((ti, tj, chan), BF16), shape((heads, chan), F32), shape((1, chan), F32),
-        ),
-        in_specs=[vmem] * 9,
+        out_shape=outs,
+        in_specs=[hbm] * 9,
         out_specs=(vmem,) * 7,
         scratch_shapes=scratch,
         compiler_params=pltpu.CompilerParams(
             collective_id=0, has_side_effects=True, vmem_limit_bytes=48 * 1024 * 1024
         ),
-    )(
-        queries[0], keys[0], values[0], out_grad[0], pair, ln_gain.reshape(1, chan), proj_weight.T,
-        token_mask.reshape(tiles, LANES), atom_map.reshape(atoms // LANES, LANES),
-    )
+    )(*(pltpu.with_memory_space_constraint(x, pltpu.HBM) for x in operands))
+    att, qg, kg, vg, pg, wg, gg = pl.pallas_call(
+        put_out,
+        out_shape=outs,
+        in_specs=[vmem] * 7,
+        out_specs=(hbm,) * 7,
+        scratch_shapes=[dma((7,))],
+        compiler_params=pltpu.CompilerParams(vmem_limit_bytes=16 * 1024 * 1024),
+    )(*results)
     return att[None], qg[None], kg[None], vg[None], pg, wg.T, gg[0]
 
 

time: 88.3 us -> 78 us (0.88)
  local copies, waits for them, and re-layouts: 9.73 us -> 0 us
    unnamed x25 -> x0, local copies, waits for them, and re-layouts: 9.73 us -> none
    pallas_call x1 -> x2, Pallas kernels: 77.4 us -> 77.2 us  [the longest x1 76.4 us: local(): pl.pallas_call(functools.partial(kernel, samp, heads, atoms), out_shape=o...]
where the time goes in v2:
time: 78 us; the launch traced here: 77.9 us
  Pallas kernels  77.2 us (99%)
    pallas_call x1, Pallas kernels, local(): pl.pallas_call(functools.partial(kernel, samp, heads, atoms), out_shape=o...  76.4 us

profile of v2, /device:TPU:1, one launch (start us, length us, event | category | flops | bytes accessed | tf_op | source)
XLA Modules:
  0.0 77.9 jit_solution(16168617131287562935)
XLA Ops:
  0.6 76.4 %shard_map.144 = (bf16[48,512]{1,0:T(8,128)(2,1)S(1)}, bf16[48,512]{1,0:T(8,128)(2,1)S(1)}, bf16[48,512]{1,0:T(8,128)(2,1)S(1)}, bf16[48,512]{1,0:T(8,128)(2,1)S...) custom-call(bf16[32,16,128]{2,1,0:T(8,128)(2,1)} %pair_hbm.1, ...), custom_call_target="tpu_custom_call" | custom-call | tf_op jit(solution)/shard_map/pallas_call | solution.py:437
  77.1 0.8 %shard_map.145 = (bf16[48,512]{1,0:T(8,128)(2,1)}, bf16[48,512]{1,0:T(8,128)(2,1)}, bf16[48,512]{1,0:T(8,128)(2,1)}, bf16[48,512]{1,0:T(8,128)(2,1)}, bf16[32,16...) custom-call(bf16[48,512]{1,0:T(8,128)(2,1)S(1)} %get-tuple-element.21.refs_0_, ...), custom_call_target="tpu_custom_call" | custom-call | tf_op jit(solution)/shard_map/pallas_call | solution.py:447

commit v3 on v2

v3 whole, which is shorter than its diff:
```python
import functools
import itertools
import math

import jax
import jax.numpy as jnp
from jax import lax
from jax.experimental import pallas as pl
from jax.experimental.pallas import tpu as pltpu
from jax.sharding import PartitionSpec as P

MESH = pl.DeviceIdType.MESH
F32 = jnp.float32
BF16 = jnp.bfloat16
LANES = 128
YH = 2


def dot_nn(a, b):
    return lax.dot_general(a, b, (((1,), (0,)), ((), ())), preferred_element_type=F32)


def dot_nt(a, b):
    return lax.dot_general(a, b, (((1,), (1,)), ((), ())), preferred_element_type=F32)


def dot_tn(a, b):
    return lax.dot_general(a, b, (((0,), (0,)), ((), ())), preferred_element_type=F32)


def kernel(
    samp, heads, atoms,
    pair_hbm, gain_hbm, w_hbm, mask_hbm, atom_hbm, g_hbm, q_hbm, k_hbm, v_hbm,
    att_ref, qg_ref, kg_ref, vg_ref, pg_ref, wg_ref, gg_ref,
    pair_ref, gain_ref, w_ref, mask_ref, atom_ref, g_ref, q_ref, k_ref, v_ref,
    ko_ref, vo_ref, qo_ref, go_ref, xs, norm, inv, ln, tile32, tsend, trecv, bias, score, dprob, probb, dsb, dsum, top,
    tx_half, rx_half, tx_whole, rx_whole,
    rin, racc, fin, brecv, part, arr1, row, arr2, tot, res,
    a_send, a_recv, ag_send, ag_recv, rs_send, rs_recv, b_send, b_recv,
    s1, r1, s2, r2, s3, r3, x_send, x_recv, y_send, y_recv, in_sem,
):
    arrays = (
        (pair_hbm, pair_ref), (gain_hbm, gain_ref), (w_hbm, w_ref), (mask_hbm, mask_ref), (atom_hbm, atom_ref),
        (k_hbm, k_ref), (v_hbm, v_ref),
    )
    feat, count = k_ref.shape
    half = count // YH
    for y in range(YH):
        arrays += ((q_hbm.at[:, y * half : (y + 1) * half], q_ref.at[y]), (g_hbm.at[:, y * half : (y + 1) * half], g_ref.at[y]))
    loads = [pltpu.make_async_copy(src, dst, in_sem.at[i]) for i, (src, dst) in enumerate(arrays)]
    for load in loads:
        load.start()
    zn = samp // YH
    plane = YH * heads
    tj, ti = count // samp, count // heads
    groups = LANES // ti
    tiles = count // LANES
    inv_root = 1.0 / math.sqrt(feat)

    me_s, me_h = lax.axis_index("samp"), lax.axis_index("head")
    yh, z = me_s // zn, lax.rem(me_s, zn)
    me_p = yh * heads + me_h
    share = heads // YH
    half_of_me = me_h // share
    mate = ((1 - yh) * zn + z, me_h)
    grp = lax.rem(me_h, groups)

    def at_plane(p):
        return (p // heads) * zn + z, lax.rem(p, heads)

    def wrap(o):
        return lax.rem(z + (o + 2 * zn), zn)

    def at_z(o):
        return yh * zn + wrap(o), me_h

    barrier = pltpu.get_barrier_semaphore()

    def greet(off, c):
        pl.semaphore_signal(barrier, inc=1, device_id=at_plane(lax.rem(me_p + off, plane)), device_id_type=MESH)
        return c

    lax.fori_loop(1, plane, greet, 0, unroll=True)
    near_far = (1, -1, 2, -2, zn // 4, -(zn // 4), zn // 2)
    for o in near_far:
        pl.semaphore_signal(barrier, inc=1, device_id=at_z(o), device_id_type=MESH)

    for load in loads[:3]:
        load.wait()

    gain = gain_ref[...]
    xs[...] = pair_ref[...].astype(F32).reshape(ti * tj, LANES)
    for j in range(tj):
        x = xs[pl.ds(j, ti, stride=tj), :]
        mu = jnp.mean(x, axis=-1, keepdims=True)
        d = x - mu
        iv = 1.0 / jnp.sqrt(jnp.mean(d * d, axis=-1, keepdims=True) + 1e-05)
        n = d * iv
        rows = slice(j * ti, (j + 1) * ti)
        norm[rows, :] = n
        inv[rows, :] = jnp.broadcast_to(iv, (ti, LANES))
        ln[rows, :] = (n * gain).astype(BF16)
    wt = w_ref[...]
    zb = dot_nt(wt, ln[...])
    lane_group = lax.broadcasted_iota(jnp.int32, (heads, LANES), 1) // ti
    for j in range(tj):
        t, jj = j // groups, j % groups
        turned = pltpu.roll(zb[:, t * LANES : (t + 1) * LANES], lax.rem(grp - jj + groups, groups) * ti, axis=1)
        tile32[pl.ds(j, heads, stride=tj), :] = jnp.where(lane_group == grp, turned, 0.0)
    tsend[...] = tile32[...].reshape(heads, tj, LANES).astype(BF16)

    pl.semaphore_wait(barrier, plane - 1 + len(near_far))

    def all_of(ref, n, sem):
        return pltpu.make_async_copy(ref.at[pl.ds(0, n)], ref.at[pl.ds(0, n)], sem)

    def plane_send(src_of, dst, send, recv):
        def body(off, c):
            p = lax.rem(me_p + off, plane)
            pltpu.make_async_remote_copy(
                src_ref=src_of(p), dst_ref=dst.at[me_p], send_sem=send, recv_sem=recv,
                device_id=at_plane(p), device_id_type=MESH,
            ).start()
            return c

        lax.fori_loop(1, plane, body, 0, unroll=True)

    slot = yh * share + lax.rem(me_h, share)

    def tile_out(h):
        return pltpu.make_async_remote_copy(
            src_ref=tsend.at[h], dst_ref=trecv.at[slot], send_sem=a_send.at[0], recv_sem=a_recv.at[0],
            device_id=(half_of_me * zn + z, h), device_id_type=MESH,
        )

    for b in range(1, heads):
        tile_out(lax.rem(me_h + b, heads)).start()

    @pl.when(half_of_me == yh)
    def _():
        pltpu.make_async_copy(tsend.at[me_h], trecv.at[slot], a_recv.at[0]).start()

    @pl.when(half_of_me != yh)
    def _():
        tile_out(me_h).start()

    for load in loads[3:]:
        load.wait()
    length = jnp.sum(mask_ref[...].astype(F32), axis=(0, 1), keepdims=True)
    step = 64

    def counting(c, carry):
        ids = lax.broadcasted_iota(jnp.int32, (step, LANES), 0) + (c * step + yh * half)
        acc = jnp.zeros((step, LANES), F32)
        for r in range(atoms // LANES):
            acc = acc + jnp.where(atom_ref[r : r + 1, :] == ids, 1.0, 0.0)
        xs[pl.ds(pl.multiple_of(c * step, step), step), :] = acc
        return carry

    lax.fori_loop(0, half // step, counting, 0)
    counts = dot_nt(jnp.ones((8, LANES), BF16), xs[0:half, :].astype(BF16))[0:1, :]
    real = (lax.broadcasted_iota(jnp.int32, (1, half), 1) + yh * half).astype(F32) < length
    tok = jnp.where(real, counts * (count / atoms), 0.0)
    chunk = LANES // tj
    top[...] = jnp.full(top.shape, -3.0e38, F32)

    def operands(sm):
        if sm:
            query, grad, key, value = qo_ref[...], go_ref[...], ko_ref[...], vo_ref[...]
        else:
            query, grad, key, value = q_ref[yh], g_ref[yh], k_ref[...], v_ref[...]
        return query, (grad.astype(F32) * tok).astype(BF16), key, value

    def raw(sm):
        query, grad, key, value = operands(sm)
        for c in range(tiles):
            cols = slice(c * LANES, (c + 1) * LANES)
            keep = lax.broadcasted_iota(jnp.int32, (LANES, 1), 0).astype(F32) + float(c * LANES) < length
            s = jnp.where(keep, dot_tn(key[:, cols], query) * inv_root, -1000000000.0)
            score[sm, c * chunk : (c + 1) * chunk] = s.reshape(chunk, tj, half)
            dprob[sm, c * chunk : (c + 1) * chunk] = dot_tn(value[:, cols], grad).reshape(chunk, tj, half)

    pltpu.make_async_copy(trecv, trecv, a_recv.at[0]).wait()
    for y in range(YH):
        for t in range(half // LANES):
            block = trecv[y * share + t * groups]
            for u in range(1, groups):
                block = block + trecv[y * share + t * groups + u]
            bias[y, z, :, t * LANES : (t + 1) * LANES] = block

    def ag_copy(sem, y, origin, o):
        return pltpu.make_async_remote_copy(
            src_ref=bias.at[y, wrap(origin)], dst_ref=bias.at[y, wrap(origin)],
            send_sem=ag_send.at[y, sem], recv_sem=ag_recv.at[y, sem], device_id=at_z(o), device_id_type=MESH,
        )

    def absorb(*origins):
        for y in range(YH):
            o = wrap(origins[(y + 1) % len(origins)])
            b = bias[y, o].astype(F32)
            for sm in range(YH):
                s = score[sm, y * zn + o] + b
                score[sm, y * zn + o] = s
                top[sm] = jnp.maximum(top[sm], jnp.max(s.reshape(tj // 8, 8, half), axis=0))

    both = range(YH)
    quarter = zn // 4
    member = (0, 2 * quarter, quarter, -quarter)

    def near(i, y):
        return (1, -1, 2 - 4 * y)[i]

    def far_copy(m, y):
        return ag_copy(m - 1, y, 0, -member[m])

    def near_copy(i, m, y):
        return ag_copy(3 + 4 * i + m, y, member[m], near(i, y))

    sent = []

    def go(copy):
        copy.start()
        sent.append(copy)

    def pass_on(m):
        for i in range(3):
            for y in both:
                go(near_copy(i, m, y))

    def take(m):
        for i in range(3):
            for y in both:
                near_copy(i, m, y).wait_recv()
        absorb(member[m] - 1)
        absorb(member[m] + 1)
        absorb(member[m] + 2, member[m] - 2)

    for m in (1, 2, 3):
        for y in both:
            go(far_copy(m, y))
    pass_on(0)

    def to_mate(src, dst, i, send, recv):
        return pltpu.make_async_remote_copy(
            src_ref=src, dst_ref=dst, send_sem=send.at[i], recv_sem=recv.at[i], device_id=mate, device_id_type=MESH,
        )

    swaps = [
        to_mate(src, dst, i, x_send, x_recv)
        for i, (src, dst) in enumerate(
            ((q_ref.at[1 - yh], qo_ref), (k_ref, ko_ref), (g_ref.at[1 - yh], go_ref), (v_ref, vo_ref))
        )
    ]
    for swap in swaps:
        go(swap)
    raw(0)
    for m in (2, 3):
        for y in both:
            far_copy(m, y).wait_recv()
        pass_on(m)
    for swap in swaps:
        swap.wait_recv()
    raw(1)
    absorb(0)
    absorb(member[2])
    absorb(member[3])
    take(0)
    for y in both:
        far_copy(1, y).wait_recv()
    pass_on(1)
    absorb(member[1])
    for m in (2, 3, 1):
        take(m)

    largest = [jnp.max(top[sm], axis=0, keepdims=True) for sm in both]

    def first(b, carry):
        new = []
        for sm in both:
            total, dots = carry[2 * sm], carry[2 * sm + 1]
            p = jnp.exp(score[sm, pl.ds(b * 2, 2)] - largest[sm][None])
            score[sm, pl.ds(b * 2, 2)] = p
            pd = p * dprob[sm, pl.ds(b * 2, 2)]
            new.append(total + jnp.sum(p.reshape(2 * tj // 8, 8, half), axis=0))
            new.append(dots + jnp.sum(pd.reshape(2 * tj // 8, 8, half), axis=0))
        return tuple(new)

    zero = jnp.zeros((8, half), F32)
    sums = lax.fori_loop(0, samp // 2, first, (zero,) * 4)
    scale = [1.0 / jnp.sum(sums[2 * sm], axis=0, keepdims=True) for sm in both]
    row_dot = [jnp.sum(sums[2 * sm + 1], axis=0, keepdims=True) * scale[sm] for sm in both]

    def second(b, carry):
        for y in both:
            both_ds = None
            for sm in both:
                prob = score[sm, y * zn + b] * scale[sm]
                probb[sm, y, b] = prob.astype(BF16)
                ds = prob * (dprob[sm, y * zn + b] - row_dot[sm])
                dsb[sm, y, b] = ds.astype(BF16)
                both_ds = ds if sm == 0 else both_ds + ds
            dsum[y, b] = both_ds.astype(BF16)
        return carry

    lax.fori_loop(0, zn, second, 0)

    def rs_copy(sem, y, src, o):
        return pltpu.make_async_remote_copy(
            src_ref=src, dst_ref=rin.at[sem, y], send_sem=rs_send.at[y, sem], recv_sem=rs_recv.at[y, sem],
            device_id=at_z(o), device_id_type=MESH,
        )

    def own(o, y):
        return dsum.at[y, wrap(o)]

    def mine(o, y):
        return dsum[y, wrap(o)].astype(F32)

    def arrived(sem, y):
        rs_copy(sem, y, own(0, y), 1).wait_recv()
        return rin[sem, y].astype(F32)

    def give(m):
        for i in range(3):
            for y in both:
                go(rs_copy(3 + 4 * i + m, y, own(near(i, y) + member[m], y), near(i, y)))

    def gather(m, y):
        return mine(member[m], y) + arrived(3 + m, y) + arrived(7 + m, y) + arrived(11 + m, y)

    def send_far(m):
        for y in both:
            racc[m - 1, y] = gather(m, y).astype(BF16)
            go(rs_copy(m - 1, y, racc.at[m - 1, y], member[m]))

    def rows_out(sm):
        query, grad, key, value = operands(sm)
        attended = dot_nn(value, probb[sm].reshape(count, half)).astype(BF16)
        query_grad = (dot_nn(key, dsb[sm].reshape(count, half)) * inv_root).astype(BF16)
        return attended, query_grad

    def columns_out(sm):
        query, grad, key, value = operands(sm)
        return dot_nt(query, dsb[sm].reshape(count, half)), dot_nt(grad, probb[sm].reshape(count, half))

    for m in (1, 2, 3):
        give(m)
    tx_half[0], tx_half[1] = rows_out(1)
    send_far(1)
    give(0)
    send_far(2)
    send_far(3)
    tx_whole[0], tx_whole[1] = columns_out(1)
    results = [
        to_mate(src, dst, i, y_send, y_recv)
        for i, (src, dst) in enumerate(((tx_half, rx_half), (tx_whole, rx_whole)))
    ]
    for result in results:
        go(result)
    att_ref[yh], qg_ref[yh] = rows_out(0)
    key_part, value_part = columns_out(0)
    for y in both:
        acc = gather(0, y) + arrived(1, y) + arrived(2, y) + arrived(0, y)
        for t in range(half // LANES):
            fin[y, t] = acc[:, t * LANES : (t + 1) * LANES].astype(BF16)

    def tile_back(dy, u):
        y = lax.rem(yh + dy, YH)
        place = lax.rem(me_h + u, share)
        return pltpu.make_async_remote_copy(
            src_ref=fin.at[y, place // groups], dst_ref=brecv.at[me_h], send_sem=b_send.at[0], recv_sem=b_recv.at[0],
            device_id=(y * zn + z, yh * share + place), device_id_type=MESH,
        )

    for dy, u in itertools.product(range(YH), range(share)):
        if dy or u:
            tile_back(dy, u).start()

    @pl.when(half_of_me == yh)
    def _():
        pltpu.make_async_copy(
            fin.at[yh, lax.rem(me_h, share) // groups], brecv.at[me_h], b_recv.at[0]
        ).start()

    @pl.when(half_of_me != yh)
    def _():
        tile_back(0, 0).start()

    pltpu.make_async_copy(brecv, brecv, b_recv.at[0]).wait()
    tile32[...] = brecv[...].astype(F32).reshape(heads * tj, LANES)
    pieces = []
    for t in range(tj // groups):
        piece = jnp.zeros((heads, LANES), F32)
        for jj in range(groups):
            r = tile32[pl.ds(t * groups + jj, heads, stride=tj), :]
            turned = pltpu.roll(r, lax.rem(jj - grp + groups, groups) * ti, axis=1)
            piece = jnp.where(lane_group == jj, turned, piece)
        pieces.append(piece)
    bg = jnp.concatenate(pieces, axis=1)
    hi = bg.astype(BF16)
    lo = (bg - hi.astype(F32)).astype(BF16)
    wpart = dot_nn(hi, ln[...]) + dot_nn(lo, ln[...])
    lng = dot_tn(hi, wt) + dot_tn(lo, wt)
    for r in range(heads):
        part[r] = wpart[r : r + 1, :]
    part[heads] = jnp.sum(lng * norm[...], axis=0, keepdims=True)
    for r in range(heads + 1, plane):
        part[r] = jnp.zeros((1, LANES), F32)

    plane_send(lambda p: part.at[p], arr1, s1.at[0], r1.at[0])
    arr1[me_p] = part[me_p]

    for j in range(tj):
        rows = slice(j * ti, (j + 1) * ti)
        n = norm[rows, :]
        dn = lng[rows, :] * gain
        out = dn - jnp.mean(dn, axis=-1, keepdims=True) - n * jnp.mean(dn * n, axis=-1, keepdims=True)
        xs[pl.ds(j, ti, stride=tj), :] = out * inv[rows, :]
    pg_ref[...] = xs[...].reshape(ti, tj, LANES).astype(BF16)

    for result in results:
        result.wait_recv()
    att_ref[1 - yh] = rx_half[0]
    qg_ref[1 - yh] = rx_half[1]
    kg_ref[...] = ((key_part + rx_whole[0]) * inv_root).astype(BF16)
    vg_ref[...] = (value_part + rx_whole[1]).astype(BF16)
    all_of(arr1, plane - 1, r1.at[0]).wait()
    row[...] = jnp.sum(arr1[...], axis=0)

    def z_send(off, c):
        pltpu.make_async_remote_copy(
            src_ref=row, dst_ref=arr2.at[z], send_sem=s2.at[0], recv_sem=r2.at[0],
            device_id=at_z(off), device_id_type=MESH,
        ).start()
        return c

    lax.fori_loop(1, zn, z_send, 0, unroll=True)
    arr2[z] = row[...]
    all_of(arr2, zn - 1, r2.at[0]).wait()
    tot[...] = jnp.sum(arr2[...], axis=0) * (1.0 / count)
    plane_send(lambda p: tot, res, s3.at[0], r3.at[0])
    res[me_p] = tot[...]
    all_of(res, plane - 1, r3.at[0]).wait()
    wg_ref[...] = jnp.concatenate([res[r] for r in range(heads)], axis=0)
    gg_ref[...] = res[heads]

    all_of(trecv, heads - 1, a_send.at[0]).wait()
    all_of(brecv, heads - 1, b_send.at[0]).wait()

    @pl.when(half_of_me != yh)
    def _():
        all_of(trecv, 1, a_send.at[0]).wait()
        all_of(brecv, 1, b_send.at[0]).wait()

    for copy in sent:
        copy.wait_send()
    all_of(arr1, plane - 1, s1.at[0]).wait()
    all_of(arr2, zn - 1, s2.at[0]).wait()
    all_of(res, plane - 1, s3.at[0]).wait()


def put_out(*refs):
    sem = refs[-1]
    half = refs[0].shape[2]
    pairs = [(refs[i].at[y], refs[7 + i].at[:, y * half : (y + 1) * half]) for i in range(2) for y in range(YH)]
    pairs += [(refs[i], refs[7 + i]) for i in range(2, 7)]
    copies = [pltpu.make_async_copy(src, dst, sem.at[i]) for i, (src, dst) in enumerate(pairs)]
    for copy in copies:
        copy.start()
    for copy in copies:
        copy.wait()


def local(samp, heads, queries, keys, values, out_grad, pair, ln_gain, proj_weight, token_mask, atom_map):
    _, feat, count = queries.shape
    ti, tj, chan = pair.shape
    atoms = atom_map.shape[0]
    zn = samp // YH
    plane = YH * heads
    tiles = count // LANES
    vmem = pl.BlockSpec(memory_space=pltpu.VMEM)
    row = (1, LANES)
    dma = pltpu.SemaphoreType.DMA
    operands = (
        pair, ln_gain.reshape(1, chan), proj_weight.T, token_mask.reshape(tiles, LANES),
        atom_map.reshape(atoms // LANES, LANES), out_grad[0], queries[0], keys[0], values[0],
    )
    half = count // YH
    halves = ((YH, feat, half), BF16)
    wide = ((feat, count), BF16)
    loaded = [(x.shape, x.dtype) for x in operands[:5]] + [halves, halves, wide, wide]
    loaded += [wide, wide, ((feat, half), BF16), ((feat, half), BF16)]
    scratch = [pltpu.VMEM(*x) for x in loaded] + [
        pltpu.VMEM((max(ti * tj, count), LANES), F32),
        pltpu.VMEM((ti * tj, LANES), F32),
        pltpu.VMEM((ti * tj, LANES), F32),
        pltpu.VMEM((ti * tj, LANES), BF16),
        pltpu.VMEM((heads * tj, LANES), F32),
        pltpu.VMEM((heads, tj, LANES), BF16),
        pltpu.VMEM((heads, tj, LANES), BF16),
        pltpu.VMEM((YH, zn, tj, half), BF16),
        pltpu.VMEM((YH, samp, tj, half), F32),
        pltpu.VMEM((YH, samp, tj, half), F32),
        pltpu.VMEM((YH, YH, zn, tj, half), BF16),
        pltpu.VMEM((YH, YH, zn, tj, half), BF16),
        pltpu.VMEM((YH, zn, tj, half), BF16),
        pltpu.VMEM((YH, 8, half), F32),
        pltpu.VMEM((2, feat, half), BF16),
        pltpu.VMEM((2, feat, half), BF16),
        pltpu.VMEM((2, feat, count), F32),
        pltpu.VMEM((2, feat, count), F32),
        pltpu.VMEM((15, YH, tj, half), BF16),
        pltpu.VMEM((3, YH, tj, half), BF16),
        pltpu.VMEM((YH, half // LANES, tj, LANES), BF16),
        pltpu.VMEM((heads, tj, LANES), BF16),
        pltpu.VMEM((plane,) + row, F32),
        pltpu.VMEM((plane,) + row, F32),
        pltpu.VMEM(row, F32),
        pltpu.VMEM((zn,) + row, F32),
        pltpu.VMEM(row, F32),
        pltpu.VMEM((plane,) + row, F32),
        dma((1,)), dma((1,)), dma((YH, 15)), dma((YH, 15)), dma((YH, 15)), dma((YH, 15)),
        dma((1,)), dma((1,)), dma((1,)), dma((1,)), dma((1,)), dma((1,)), dma((1,)), dma((1,)), dma((4,)), dma((4,)), dma((2,)), dma((2,)), dma((11,)),
    ]
    shape = jax.ShapeDtypeStruct
    tail = (
        shape((feat, count), BF16), shape((feat, count), BF16), shape((ti, tj, chan), BF16),
        shape((heads, chan), F32), shape((1, chan), F32),
    )
    outs = (shape((feat, count), BF16),) * 2 + tail
    hbm = pl.BlockSpec(memory_space=pltpu.HBM)
    results = pl.pallas_call(
        functools.partial(kernel, samp, heads, atoms),
        out_shape=(shape((YH, feat, half), BF16),) * 2 + tail,
        in_specs=[hbm] * 9,
        out_specs=(vmem,) * 7,
        scratch_shapes=scratch,
        compiler_params=pltpu.CompilerParams(
            collective_id=0, has_side_effects=True, vmem_limit_bytes=48 * 1024 * 1024
        ),
    )(*(pltpu.with_memory_space_constraint(x, pltpu.HBM) for x in operands))
    att, qg, kg, vg, pg, wg, gg = pl.pallas_call(
        put_out,
        out_shape=outs,
        in_specs=[vmem] * 7,
        out_specs=(hbm,) * 7,
        scratch_shapes=[dma((9,))],
        compiler_params=pltpu.CompilerParams(vmem_limit_bytes=16 * 1024 * 1024),
    )(*results)
    return att[None], qg[None], kg[None], vg[None], pg, wg.T, gg[0]


def solution(mesh):
    cut = P("samp", "head", None)
    return jax.shard_map(
        functools.partial(local, mesh.shape["samp"], mesh.shape["head"]),
        mesh=mesh,
        in_specs=(cut, cut, cut, cut, P("head", "samp", None), P(), P(), P(), P()),
        out_specs=(cut, cut, cut, cut, P("head", "samp", None), P(), P()),
        check_vma=False,
    )
```

time: 78 us -> 69.6 us (0.89)
  Pallas kernels: 77.2 us -> 68.9 us
    pallas_call x1, Pallas kernels: 76.4 us -> 68.1 us  [local(): pl.pallas_call(functools.partial(kernel, samp, heads, atoms), out_shape=(...]
where the time goes in v3:
time: 69.6 us; the launch traced here: 69.5 us
  Pallas kernels  68.9 us (99%)
    pallas_call x1, Pallas kernels, local(): pl.pallas_call(functools.partial(kernel, samp, heads, atoms), out_shape=(...  68.1 us

profile of v3, /device:TPU:1, one launch (start us, length us, event | category | flops | bytes accessed | tf_op | source)
XLA Modules:
  0.0 69.5 jit_solution(10786166261524362723)
XLA Ops:
  0.6 68.1 %shard_map.144 = (bf16[2,48,256]{2,1,0:T(8,128)(2,1)S(1)}, bf16[2,48,256]{2,1,0:T(8,128)(2,1)S(1)}, bf16[48,512]{1,0:T(8,128)(2,1)S(1)}, bf16[48,512]{1,0:T(8,12...) custom-call(bf16[32,16,128]{2,1,0:T(8,128)(2,1)} %pair_hbm.1, ...), custom_call_target="tpu_custom_call" | custom-call | tf_op jit(solution)/shard_map/pallas_call | solution.py:532
  68.7 0.8 %shard_map.145 = (bf16[48,512]{1,0:T(8,128)(2,1)}, bf16[48,512]{1,0:T(8,128)(2,1)}, bf16[48,512]{1,0:T(8,128)(2,1)}, bf16[48,512]{1,0:T(8,128)(2,1)}, bf16[32,16...) custom-call(bf16[2,48,256]{2,1,0:T(8,128)(2,1)S(1)} %get-tuple-element.21.refs_0_, ...), custom_call_target="tpu_custom_call" | custom-call | tf_op jit(solution)/shard_map/pallas_call | solution.py:542

commit v4 on v3

--- a/solution.py
+++ b/solution.py
@@ -37,7 +37,7 @@
     tx_half, rx_half, tx_whole, rx_whole,
     rin, racc, fin, brecv, part, arr1, row, arr2, tot, res,
     a_send, a_recv, ag_send, ag_recv, rs_send, rs_recv, b_send, b_recv,
-    s1, r1, s2, r2, s3, r3, x_send, x_recv, y_send, y_recv, in_sem,
+    s1, r1, s2, r2, s3, r3, x_send, x_recv, y_send, y_recv, in_sem, word,
 ):
     arrays = (
         (pair_hbm, pair_ref), (gain_hbm, gain_ref), (w_hbm, w_ref), (mask_hbm, mask_ref), (atom_hbm, atom_ref),
@@ -65,24 +65,46 @@
     mate = ((1 - yh) * zn + z, me_h)
     grp = lax.rem(me_h, groups)
 
-    def at_plane(p):
-        return (p // heads) * zn + z, lax.rem(p, heads)
+    along = heads // 4
+
+    def turn(at, by, size):
+        return jnp.where(at + by >= size, at + by - size, at + by)
+
+    low, core = me_h // (heads // 2), lax.rem(me_h, 2)
+    across = lax.rem(me_h // 2, along)
+    row_of = [turn(low, d, 2) * (heads // 2) for d in range(2)]
+    col_of = [turn(across, d, along) * 2 for d in range(along)]
+    core_of = [turn(core, d, 2) for d in range(2)]
+    high_of = [turn(yh, d, 2) for d in range(2)]
+    samp_of = [h * zn + z for h in high_of]
+    base_of = [h * heads for h in high_of]
+
+    def steps(place):
+        high, lo, x, c = place
+        return (1 if lo else 2 * high) + min(x, along - x) + 0.1 * c
+
+    places = sorted(itertools.product(range(2), range(2), range(along), range(2)), key=steps, reverse=True)[:-1]
+
+    def head_at(lo, x, c):
+        return row_of[lo] + col_of[x] + core_of[c]
+
+    def at_place(place):
+        high, lo, x, c = place
+        return samp_of[high], head_at(lo, x, c)
 
     def wrap(o):
-        return lax.rem(z + (o + 2 * zn), zn)
+        by = o % zn
+        return turn(z, by, zn) if by else z
 
     def at_z(o):
         return yh * zn + wrap(o), me_h
 
     barrier = pltpu.get_barrier_semaphore()
 
-    def greet(off, c):
-        pl.semaphore_signal(barrier, inc=1, device_id=at_plane(lax.rem(me_p + off, plane)), device_id_type=MESH)
-        return c
-
-    lax.fori_loop(1, plane, greet, 0, unroll=True)
-    near_far = (1, -1, 2, -2, zn // 4, -(zn // 4), zn // 2)
-    for o in near_far:
+    for place in places:
+        pl.semaphore_signal(barrier, inc=1, device_id=at_place(place), device_id_type=MESH)
+    close = (1, -1, 2, -2)
+    for o in close:
         pl.semaphore_signal(barrier, inc=1, device_id=at_z(o), device_id_type=MESH)
 
     for load in loads[:3]:
@@ -109,21 +131,20 @@
         tile32[pl.ds(j, heads, stride=tj), :] = jnp.where(lane_group == grp, turned, 0.0)
     tsend[...] = tile32[...].reshape(heads, tj, LANES).astype(BF16)
 
-    pl.semaphore_wait(barrier, plane - 1 + len(near_far))
+    pl.semaphore_wait(barrier, plane - 1 + len(close))
+    for o in (2, -2):
+        pl.semaphore_signal(word.at[0], inc=1, device_id=at_z(o), device_id_type=MESH)
 
     def all_of(ref, n, sem):
         return pltpu.make_async_copy(ref.at[pl.ds(0, n)], ref.at[pl.ds(0, n)], sem)
 
     def plane_send(src_of, dst, send, recv):
-        def body(off, c):
-            p = lax.rem(me_p + off, plane)
+        for place in places:
+            samp_id, head_id = at_place(place)
             pltpu.make_async_remote_copy(
-                src_ref=src_of(p), dst_ref=dst.at[me_p], send_sem=send, recv_sem=recv,
-                device_id=at_plane(p), device_id_type=MESH,
+                src_ref=src_of(base_of[place[0]] + head_id), dst_ref=dst.at[me_p], send_sem=send, recv_sem=recv,
+                device_id=(samp_id, head_id), device_id_type=MESH,
             ).start()
-            return c
-
-        lax.fori_loop(1, plane, body, 0, unroll=True)
 
     slot = yh * share + lax.rem(me_h, share)
 
@@ -133,8 +154,9 @@
             device_id=(half_of_me * zn + z, h), device_id_type=MESH,
         )
 
-    for b in range(1, heads):
-        tile_out(lax.rem(me_h + b, heads)).start()
+    beside = [place[1:] for place in places if not place[0]]
+    for place in beside:
+        tile_out(head_at(*place)).start()
 
     @pl.when(half_of_me == yh)
     def _():
@@ -143,6 +165,10 @@
     @pl.when(half_of_me != yh)
     def _():
         tile_out(me_h).start()
+
+    pl.semaphore_wait(word.at[0], 2)
+    for o in (4, -4):
+        pl.semaphore_signal(word.at[1], inc=1, device_id=at_z(o), device_id_type=MESH)
 
     for load in loads[3:]:
         load.wait()
@@ -235,9 +261,16 @@
         absorb(member[m] + 1)
         absorb(member[m] + 2, member[m] - 2)
 
-    for m in (1, 2, 3):
+    pl.semaphore_wait(word.at[1], 2)
+    def direct_copy(i, y):
+        return ag_copy(4 + 4 * i, y, 0, member[1] + near(i, y))
+
+    for m in (2, 3, 1):
         for y in both:
             go(far_copy(m, y))
+    for i in range(3):
+        for y in both:
+            go(direct_copy(i, y))
     pass_on(0)
 
     def to_mate(src, dst, i, send, recv):
@@ -267,7 +300,6 @@
     take(0)
     for y in both:
         far_copy(1, y).wait_recv()
-    pass_on(1)
     absorb(member[1])
     for m in (2, 3, 1):
         take(m)
@@ -323,15 +355,19 @@
     def give(m):
         for i in range(3):
             for y in both:
-                go(rs_copy(3 + 4 * i + m, y, own(near(i, y) + member[m], y), near(i, y)))
+                o = near(i, y)
+                go(rs_copy(3 + 4 * i + m, y, own(o + member[m], y), o + member[1] if m == 1 else o))
 
     def gather(m, y):
         return mine(member[m], y) + arrived(3 + m, y) + arrived(7 + m, y) + arrived(11 + m, y)
 
     def send_far(m):
         for y in both:
-            racc[m - 1, y] = gather(m, y).astype(BF16)
-            go(rs_copy(m - 1, y, racc.at[m - 1, y], member[m]))
+            if m == 1:
+                go(rs_copy(0, y, own(member[1], y), member[1]))
+            else:
+                racc[m - 1, y] = gather(m, y).astype(BF16)
+                go(rs_copy(m - 1, y, racc.at[m - 1, y], member[m]))
 
     def rows_out(sm):
         query, grad, key, value = operands(sm)
@@ -343,11 +379,12 @@
         query, grad, key, value = operands(sm)
         return dot_nt(query, dsb[sm].reshape(count, half)), dot_nt(grad, probb[sm].reshape(count, half))
 
-    for m in (1, 2, 3):
-        give(m)
+    give(2)
+    give(3)
+    send_far(1)
+    give(1)
+    give(0)
     tx_half[0], tx_half[1] = rows_out(1)
-    send_far(1)
-    give(0)
     send_far(2)
     send_far(3)
     tx_whole[0], tx_whole[1] = columns_out(1)
@@ -360,21 +397,21 @@
     att_ref[yh], qg_ref[yh] = rows_out(0)
     key_part, value_part = columns_out(0)
     for y in both:
-        acc = gather(0, y) + arrived(1, y) + arrived(2, y) + arrived(0, y)
+        acc = gather(0, y) + arrived(1, y) + arrived(2, y) + arrived(0, y) + arrived(4, y) + arrived(8, y) + arrived(12, y)
         for t in range(half // LANES):
             fin[y, t] = acc[:, t * LANES : (t + 1) * LANES].astype(BF16)
 
-    def tile_back(dy, u):
-        y = lax.rem(yh + dy, YH)
-        place = lax.rem(me_h + u, share)
+    def tile_back(high, x, c):
+        spot = col_of[x] + core_of[c]
         return pltpu.make_async_remote_copy(
-            src_ref=fin.at[y, place // groups], dst_ref=brecv.at[me_h], send_sem=b_send.at[0], recv_sem=b_recv.at[0],
-            device_id=(y * zn + z, yh * share + place), device_id_type=MESH,
+            src_ref=fin.at[high_of[high], spot // groups], dst_ref=brecv.at[me_h],
+            send_sem=b_send.at[0], recv_sem=b_recv.at[0],
+            device_id=(samp_of[high], yh * share + spot), device_id_type=MESH,
         )
 
-    for dy, u in itertools.product(range(YH), range(share)):
-        if dy or u:
-            tile_back(dy, u).start()
+    for high, lo, x, c in places:
+        if not lo:
+            tile_back(high, x, c).start()
 
     @pl.when(half_of_me == yh)
     def _():
@@ -384,7 +421,7 @@
 
     @pl.when(half_of_me != yh)
     def _():
-        tile_back(0, 0).start()
+        tile_back(0, 0, 0).start()
 
     pltpu.make_async_copy(brecv, brecv, b_recv.at[0]).wait()
     tile32[...] = brecv[...].astype(F32).reshape(heads * tj, LANES)
@@ -427,14 +464,11 @@
     all_of(arr1, plane - 1, r1.at[0]).wait()
     row[...] = jnp.sum(arr1[...], axis=0)
 
-    def z_send(off, c):
+    for off in sorted(range(1, zn), key=lambda o: -min(o, zn - o)):
         pltpu.make_async_remote_copy(
             src_ref=row, dst_ref=arr2.at[z], send_sem=s2.at[0], recv_sem=r2.at[0],
             device_id=at_z(off), device_id_type=MESH,
         ).start()
-        return c
-
-    lax.fori_loop(1, zn, z_send, 0, unroll=True)
     arr2[z] = row[...]
     all_of(arr2, zn - 1, r2.at[0]).wait()
     tot[...] = jnp.sum(arr2[...], axis=0) * (1.0 / count)
@@ -520,7 +554,7 @@
         pltpu.VMEM(row, F32),
         pltpu.VMEM((plane,) + row, F32),
         dma((1,)), dma((1,)), dma((YH, 15)), dma((YH, 15)), dma((YH, 15)), dma((YH, 15)),
-        dma((1,)), dma((1,)), dma((1,)), dma((1,)), dma((1,)), dma((1,)), dma((1,)), dma((1,)), dma((4,)), dma((4,)), dma((2,)), dma((2,)), dma((11,)),
+        dma((1,)), dma((1,)), dma((1,)), dma((1,)), dma((1,)), dma((1,)), dma((1,)), dma((1,)), dma((4,)), dma((4,)), dma((2,)), dma((2,)), dma((11,)), pltpu.SemaphoreType.REGULAR((2,)),
     ]
     shape = jax.ShapeDtypeStruct
     tail = (

time: 69.6 us -> 67.2 us (0.966)
  Pallas kernels: 68.9 us -> 66.5 us
    pallas_call x1, Pallas kernels: 68.1 us -> 65.6 us  [local(): pl.pallas_call(functools.partial(kernel, samp, heads, atoms), out_shape=(...]
where the time goes in v4:
time: 67.2 us; the launch traced here: 67.1 us
  Pallas kernels  66.5 us (99%)
    pallas_call x1, Pallas kernels, local(): pl.pallas_call(functools.partial(kernel, samp, heads, atoms), out_shape=(...  65.6 us

profile of v4, /device:TPU:1, one launch (start us, length us, event | category | flops | bytes accessed | tf_op | source)
XLA Modules:
  0.0 67.1 jit_solution(10051586135265020192)
XLA Ops:
  0.6 65.6 %shard_map.144 = (bf16[2,48,256]{2,1,0:T(8,128)(2,1)S(1)}, bf16[2,48,256]{2,1,0:T(8,128)(2,1)S(1)}, bf16[48,512]{1,0:T(8,128)(2,1)S(1)}, bf16[48,512]{1,0:T(8,12...) custom-call(bf16[32,16,128]{2,1,0:T(8,128)(2,1)} %pair_hbm.1, ...), custom_call_target="tpu_custom_call" | custom-call | tf_op jit(solution)/shard_map/pallas_call | solution.py:566
  66.3 0.8 %shard_map.145 = (bf16[48,512]{1,0:T(8,128)(2,1)}, bf16[48,512]{1,0:T(8,128)(2,1)}, bf16[48,512]{1,0:T(8,128)(2,1)}, bf16[48,512]{1,0:T(8,128)(2,1)}, bf16[32,16...) custom-call(bf16[2,48,256]{2,1,0:T(8,128)(2,1)S(1)} %get-tuple-element.21.refs_0_, ...), custom_call_target="tpu_custom_call" | custom-call | tf_op jit(solution)/shard_map/pallas_call | solution.py:576

commit v5 on v4

--- a/solution.py
+++ b/solution.py
@@ -230,17 +230,9 @@
                 top[sm] = jnp.maximum(top[sm], jnp.max(s.reshape(tj // 8, 8, half), axis=0))
 
     both = range(YH)
-    quarter = zn // 4
-    member = (0, 2 * quarter, quarter, -quarter)
-
-    def near(i, y):
-        return (1, -1, 2 - 4 * y)[i]
-
-    def far_copy(m, y):
-        return ag_copy(m - 1, y, 0, -member[m])
-
-    def near_copy(i, m, y):
-        return ag_copy(3 + 4 * i + m, y, member[m], near(i, y))
+
+    def put(d, y, origin=0):
+        return ag_copy(d + 7, y, origin, origin + d)
 
     sent = []
 
@@ -248,30 +240,21 @@
         copy.start()
         sent.append(copy)
 
-    def pass_on(m):
-        for i in range(3):
+    def pass_on(side):
+        for d in (7, 6, 5, 3):
             for y in both:
-                go(near_copy(i, m, y))
-
-    def take(m):
-        for i in range(3):
+                go(put(side * d, y, -4 * side))
+
+    def take(*ds):
+        for d in ds:
             for y in both:
-                near_copy(i, m, y).wait_recv()
-        absorb(member[m] - 1)
-        absorb(member[m] + 1)
-        absorb(member[m] + 2, member[m] - 2)
+                put(d, y).wait_recv()
+            absorb(-d)
 
     pl.semaphore_wait(word.at[1], 2)
-    def direct_copy(i, y):
-        return ag_copy(4 + 4 * i, y, 0, member[1] + near(i, y))
-
-    for m in (2, 3, 1):
+    for d in (4, -4, 8, 2, -2, 1, -1):
         for y in both:
-            go(far_copy(m, y))
-    for i in range(3):
-        for y in both:
-            go(direct_copy(i, y))
-    pass_on(0)
+            go(put(d, y))
 
     def to_mate(src, dst, i, send, recv):
         return pltpu.make_async_remote_copy(
@@ -287,22 +270,17 @@
     for swap in swaps:
         go(swap)
     raw(0)
-    for m in (2, 3):
+    for side in (1, -1):
         for y in both:
-            far_copy(m, y).wait_recv()
-        pass_on(m)
+            put(4 * side, y).wait_recv()
+        pass_on(side)
     for swap in swaps:
         swap.wait_recv()
     raw(1)
     absorb(0)
-    absorb(member[2])
-    absorb(member[3])
-    take(0)
-    for y in both:
-        far_copy(1, y).wait_recv()
-    absorb(member[1])
-    for m in (2, 3, 1):
-        take(m)
+    absorb(-4)
+    absorb(4)
+    take(1, -1, 2, -2, 3, -3, 8, 5, -5, 6, -6, 7, -7)
 
     largest = [jnp.max(top[sm], axis=0, keepdims=True) for sm in both]
 
@@ -352,22 +330,17 @@
         rs_copy(sem, y, own(0, y), 1).wait_recv()
         return rin[sem, y].astype(F32)
 
-    def give(m):
-        for i in range(3):
-            for y in both:
-                o = near(i, y)
-                go(rs_copy(3 + 4 * i + m, y, own(o + member[m], y), o + member[1] if m == 1 else o))
-
-    def gather(m, y):
-        return mine(member[m], y) + arrived(3 + m, y) + arrived(7 + m, y) + arrived(11 + m, y)
-
-    def send_far(m):
+    def give(d, hop):
         for y in both:
-            if m == 1:
-                go(rs_copy(0, y, own(member[1], y), member[1]))
-            else:
-                racc[m - 1, y] = gather(m, y).astype(BF16)
-                go(rs_copy(m - 1, y, racc.at[m - 1, y], member[m]))
+            go(rs_copy(d + 7, y, own(d, y), hop))
+
+    def relay(side):
+        for y in both:
+            acc = mine(4 * side, y)
+            for d in (3, 5, 6, 7):
+                acc = acc + arrived(side * d + 7, y)
+            racc[(side + 1) // 2, y] = acc.astype(BF16)
+            go(rs_copy(4 * side + 7, y, racc.at[(side + 1) // 2, y], 4 * side))
 
     def rows_out(sm):
         query, grad, key, value = operands(sm)
@@ -379,14 +352,14 @@
         query, grad, key, value = operands(sm)
         return dot_nt(query, dsb[sm].reshape(count, half)), dot_nt(grad, probb[sm].reshape(count, half))
 
-    give(2)
-    give(3)
-    send_far(1)
-    give(1)
-    give(0)
+    for d, hop in ((7, 3), (6, 2), (5, 1), (3, -1)):
+        give(d, hop)
+        give(-d, -hop)
+    for d in (8, 2, -2, 1, -1):
+        give(d, d)
     tx_half[0], tx_half[1] = rows_out(1)
-    send_far(2)
-    send_far(3)
+    relay(1)
+    relay(-1)
     tx_whole[0], tx_whole[1] = columns_out(1)
     results = [
         to_mate(src, dst, i, y_send, y_recv)
@@ -397,7 +370,9 @@
     att_ref[yh], qg_ref[yh] = rows_out(0)
     key_part, value_part = columns_out(0)
     for y in both:
-        acc = gather(0, y) + arrived(1, y) + arrived(2, y) + arrived(0, y) + arrived(4, y) + arrived(8, y) + arrived(12, y)
+        acc = mine(0, y)
+        for d in (1, -1, 2, -2, 8, 4, -4):
+            acc = acc + arrived(d + 7, y)
         for t in range(half // LANES):
             fin[y, t] = acc[:, t * LANES : (t + 1) * LANES].astype(BF16)
 
@@ -543,8 +518,8 @@
         pltpu.VMEM((2, feat, half), BF16),
         pltpu.VMEM((2, feat, count), F32),
         pltpu.VMEM((2, feat, count), F32),
-        pltpu.VMEM((15, YH, tj, half), BF16),
-        pltpu.VMEM((3, YH, tj, half), BF16),
+        pltpu.VMEM((16, YH, tj, half), BF16),
+        pltpu.VMEM((2, YH, tj, half), BF16),
         pltpu.VMEM((YH, half // LANES, tj, LANES), BF16),
         pltpu.VMEM((heads, tj, LANES), BF16),
         pltpu.VMEM((plane,) + row, F32),
@@ -553,7 +528,7 @@
         pltpu.VMEM((zn,) + row, F32),
         pltpu.VMEM(row, F32),
         pltpu.VMEM((plane,) + row, F32),
-        dma((1,)), dma((1,)), dma((YH, 15)), dma((YH, 15)), dma((YH, 15)), dma((YH, 15)),
+        dma((1,)), dma((1,)), dma((YH, 16)), dma((YH, 16)), dma((YH, 16)), dma((YH, 16)),
         dma((1,)), dma((1,)), dma((1,)), dma((1,)), dma((1,)), dma((1,)), dma((1,)), dma((1,)), dma((4,)), dma((4,)), dma((2,)), dma((2,)), dma((11,)), pltpu.SemaphoreType.REGULAR((2,)),
     ]
     shape = jax.ShapeDtypeStruct

time: 67.2 us -> 65.7 us (0.978)
  Pallas kernels: 66.5 us -> 64.9 us
    pallas_call x1, Pallas kernels: 65.6 us -> 64.1 us  [local(): pl.pallas_call(functools.partial(kernel, samp, heads, atoms), out_shape=(...]
where the time goes in v5:
time: 65.7 us; the launch traced here: 65.5 us
  Pallas kernels  64.9 us (99%)
    pallas_call x1, Pallas kernels, local(): pl.pallas_call(functools.partial(kernel, samp, heads, atoms), out_shape=(...  64.1 us

profile of v5, /device:TPU:1, one launch (start us, length us, event | category | flops | bytes accessed | tf_op | source)
XLA Modules:
  0.0 65.5 jit_solution(5973448345510905846)
XLA Ops:
  0.6 64.1 %shard_map.144 = (bf16[2,48,256]{2,1,0:T(8,128)(2,1)S(1)}, bf16[2,48,256]{2,1,0:T(8,128)(2,1)S(1)}, bf16[48,512]{1,0:T(8,128)(2,1)S(1)}, bf16[48,512]{1,0:T(8,12...) custom-call(bf16[32,16,128]{2,1,0:T(8,128)(2,1)} %pair_hbm.1, ...), custom_call_target="tpu_custom_call" | custom-call | tf_op jit(solution)/shard_map/pallas_call | solution.py:541
  64.7 0.8 %shard_map.145 = (bf16[48,512]{1,0:T(8,128)(2,1)}, bf16[48,512]{1,0:T(8,128)(2,1)}, bf16[48,512]{1,0:T(8,128)(2,1)}, bf16[48,512]{1,0:T(8,128)(2,1)}, bf16[32,16...) custom-call(bf16[2,48,256]{2,1,0:T(8,128)(2,1)S(1)} %get-tuple-element.21.refs_0_, ...), custom_call_target="tpu_custom_call" | custom-call | tf_op jit(solution)/shard_map/pallas_call | solution.py:551

commit v6 on v5

--- a/solution.py
+++ b/solution.py
@@ -170,6 +170,8 @@
     for o in (4, -4):
         pl.semaphore_signal(word.at[1], inc=1, device_id=at_z(o), device_id_type=MESH)
 
+    for r in range(heads + 1, plane):
+        part[r] = jnp.zeros((1, LANES), F32)
     for load in loads[3:]:
         load.wait()
     length = jnp.sum(mask_ref[...].astype(F32), axis=(0, 1), keepdims=True)
@@ -416,8 +418,6 @@
     for r in range(heads):
         part[r] = wpart[r : r + 1, :]
     part[heads] = jnp.sum(lng * norm[...], axis=0, keepdims=True)
-    for r in range(heads + 1, plane):
-        part[r] = jnp.zeros((1, LANES), F32)
 
     plane_send(lambda p: part.at[p], arr1, s1.at[0], r1.at[0])
     arr1[me_p] = part[me_p]
@@ -436,6 +436,16 @@
     qg_ref[1 - yh] = rx_half[1]
     kg_ref[...] = ((key_part + rx_whole[0]) * inv_root).astype(BF16)
     vg_ref[...] = (value_part + rx_whole[1]).astype(BF16)
+    all_of(trecv, heads - 1, a_send.at[0]).wait()
+    all_of(brecv, heads - 1, b_send.at[0]).wait()
+
+    @pl.when(half_of_me != yh)
+    def _():
+        all_of(trecv, 1, a_send.at[0]).wait()
+        all_of(brecv, 1, b_send.at[0]).wait()
+
+    for copy in sent:
+        copy.wait_send()
     all_of(arr1, plane - 1, r1.at[0]).wait()
     row[...] = jnp.sum(arr1[...], axis=0)
 
@@ -453,16 +463,6 @@
     wg_ref[...] = jnp.concatenate([res[r] for r in range(heads)], axis=0)
     gg_ref[...] = res[heads]
 
-    all_of(trecv, heads - 1, a_send.at[0]).wait()
-    all_of(brecv, heads - 1, b_send.at[0]).wait()
-
-    @pl.when(half_of_me != yh)
-    def _():
-        all_of(trecv, 1, a_send.at[0]).wait()
-        all_of(brecv, 1, b_send.at[0]).wait()
-
-    for copy in sent:
-        copy.wait_send()
     all_of(arr1, plane - 1, s1.at[0]).wait()
     all_of(arr2, zn - 1, s2.at[0]).wait()
     all_of(res, plane - 1, s3.at[0]).wait()

time: 65.7 us -> 65.6 us (level)
  no operation moved by 1% of the time
where the time goes in v6:
time: 65.6 us; the launch traced here: 65.4 us
  Pallas kernels  64.8 us (99%)
    pallas_call x1, Pallas kernels, local(): pl.pallas_call(functools.partial(kernel, samp, heads, atoms), out_shape=(...  64 us

profile of v6, /device:TPU:1, one launch (start us, length us, event | category | flops | bytes accessed | tf_op | source)
XLA Modules:
  0.0 65.4 jit_solution(7802285879749278326)
XLA Ops:
  0.6 64.0 %shard_map.144 = (bf16[2,48,256]{2,1,0:T(8,128)(2,1)S(1)}, bf16[2,48,256]{2,1,0:T(8,128)(2,1)S(1)}, bf16[48,512]{1,0:T(8,128)(2,1)S(1)}, bf16[48,512]{1,0:T(8,12...) custom-call(bf16[32,16,128]{2,1,0:T(8,128)(2,1)} %pair_hbm.1, ...), custom_call_target="tpu_custom_call" | custom-call | tf_op jit(solution)/shard_map/pallas_call | solution.py:541
  64.6 0.8 %shard_map.145 = (bf16[48,512]{1,0:T(8,128)(2,1)}, bf16[48,512]{1,0:T(8,128)(2,1)}, bf16[48,512]{1,0:T(8,128)(2,1)}, bf16[48,512]{1,0:T(8,128)(2,1)}, bf16[32,16...) custom-call(bf16[2,48,256]{2,1,0:T(8,128)(2,1)S(1)} %get-tuple-element.21.refs_0_, ...), custom_call_target="tpu_custom_call" | custom-call | tf_op jit(solution)/shard_map/pallas_call | solution.py:551
